TPU v7x, 768 devices: a whole 4x8x12 slice. The times are simulated.
768 devices in a mesh: ep: 32 (over y, x), grp: 24 (over z, core).
Axes of the slice: x: 4, y: 8, z: 12, core: 2. Of those that a mesh axis runs over, the one named last changes fastest.
Arguments:
- token_inputs: bfloat16 [98304, 768], P(('ep', 'grp')), may hold values from -6 to 6
- output_grads: bfloat16 [98304, 768], P(('ep', 'grp')), may hold values from -6 to 6
- gate_probs: float32 [98304], P(('ep', 'grp')), may hold values from 0.2 to 1
- token_slots: int32 [98304], replicated, may hold values from 0 to 767, as said below
- slot_experts: int32 [32, 24], P('ep'), may hold values from 0 to 127, as said below
- slot_capacity: int32 [32, 24], P('ep', 'grp'), may hold values from 64 to 256, as said below
- weight_in: bfloat16 [32, 24, 768, 1024], P('ep', 'grp'), as said below
- weight_out: bfloat16 [32, 24, 768, 1024], P('ep', 'grp'), as said below
Outputs:
- input_grads: bfloat16 [98304, 768], P(('ep', 'grp'))
- expert_grads: bfloat16 [2, 128, 768, 1024], P(None, 'ep', 'grp')
Inputs may be any that keep to these rules, and one draw needn't show every extreme that they name: `token_slots`: tokens stand in blocks of 128, one block for each device in the order ep then grp. Of one block's tokens at most 8 go to slots of one grp index; for every ep index, one grp index takes exactly 8 from every block of that ep index. Of the tokens of all blocks of one ep index bound for one grp index, at most 8 go to any one slot, and exactly 8 in some cases. `slot_experts`: the 24 slots of ep index c host experts c * 4 to c * 4 + 3, each on 1 to 8 slots, and one of them in every column on exactly 8 slots. `slot_capacity`: some slot has capacity 256. `weight_in`: the copies on all slots that host one expert are equal. `weight_out`: the copies on all slots that host one expert are equal.
All inputs are finite; a program needn't handle non-finite values.
Results may differ from a plain program's by a relative error of at most 0.0064.
Values may be sent and summed in bfloat16 or wider, within the bound.
No kernel may reach another device: no remote copies, remote signals or barrier semaphores. Data moves between devices by JAX's collectives and lax.ppermute only.
A program may use at most 32 MiB of HBM per device.

v0:
```python
import jax
import jax.numpy as jnp
from jax import lax
from jax.sharding import PartitionSpec as P

EXP_COL = 4


coef_a = 0.7978845608028654
coef_b = 0.044715


def gelu_pair(preact):
    square = preact * preact
    tanh_value = jnp.tanh(coef_a * preact * (1.0 + coef_b * square))
    half_sum = 0.5 * (1.0 + tanh_value)
    gelu_value = preact * half_sum
    gelu_slope = half_sum + 0.5 * preact * (1.0 - tanh_value * tanh_value) * coef_a * (
        1.0 + 3.0 * coef_b * square
    )
    return (gelu_value, gelu_slope)


def padded_take(source, take_index):
    filler = jnp.zeros((1,) + source.shape[1:], source.dtype)
    return jnp.concatenate([source, filler], axis=0)[take_index]


def slot_work(compact_index, inputs_flat, grads_flat, first_weight, second_weight):
    slot_inputs = padded_take(inputs_flat, compact_index)
    slot_grads = padded_take(grads_flat, compact_index)
    preact = jnp.dot(slot_inputs, first_weight, preferred_element_type=jnp.float32)
    gelu_value, gelu_slope = gelu_pair(preact)
    activated = gelu_value.astype(jnp.bfloat16)
    hidden_grad = jnp.dot(slot_grads, second_weight, preferred_element_type=jnp.float32)
    preact_grad = (hidden_grad * gelu_slope).astype(jnp.bfloat16)
    row_grads = lax.dot_general(
        preact_grad, first_weight, (((1,), (1,)), ((), ())), preferred_element_type=jnp.float32
    ).astype(jnp.bfloat16)
    grad_in = lax.dot_general(
        slot_inputs, preact_grad, (((0,), (0,)), ((), ())), preferred_element_type=jnp.float32
    ).astype(jnp.bfloat16)
    grad_out = lax.dot_general(
        slot_grads, activated, (((0,), (0,)), ((), ())), preferred_element_type=jnp.float32
    ).astype(jnp.bfloat16)
    return (row_grads, grad_in, grad_out)


def per_device(
    token_inputs,
    output_grads,
    gate_probs,
    token_slots,
    slot_experts,
    slot_capacity,
    weight_in,
    weight_out,
):
    ep_count = lax.axis_size("ep")
    grp_count = lax.axis_size("grp")
    ep_index = lax.axis_index("ep")
    grp_index = lax.axis_index("grp")
    tok_dev, model_width = token_inputs.shape
    hidden = weight_in.shape[3]
    row_cap = 8 * ((3 * tok_dev + 16 * grp_count - 1) // (16 * grp_count))
    col_cap = 8 * ((grp_count * row_cap + 8 * ep_count - 1) // (8 * ep_count))
    cap_max = 2 * tok_dev
    first_weight = weight_in.reshape(model_width, hidden)
    second_weight = weight_out.reshape(model_width, hidden)
    scaled = (gate_probs[:, None] * output_grads.astype(jnp.float32)).astype(jnp.bfloat16)
    own_start = (ep_index * grp_count + grp_index) * tok_dev
    own_slots = lax.dynamic_slice_in_dim(token_slots, own_start, tok_dev)
    dest_rows = own_slots % grp_count
    row_onehot = (dest_rows[:, None] == jnp.arange(grp_count, dtype=jnp.int32)[None, :]).astype(
        jnp.int32
    )
    row_place = jnp.sum(jnp.cumsum(row_onehot, axis=0) * row_onehot, axis=1) - 1
    send_place = dest_rows * row_cap + row_place
    send_index = (
        jnp.full((grp_count * row_cap,), tok_dev, jnp.int32)
        .at[send_place]
        .set(jnp.arange(tok_dev, dtype=jnp.int32))
    )
    inputs_out = padded_take(token_inputs, send_index).reshape(grp_count, row_cap, model_width)
    grads_out = padded_take(scaled, send_index).reshape(grp_count, row_cap, model_width)
    inputs_mid, grads_mid = (
        lax.all_to_all(inputs_out, "grp", split_axis=0, concat_axis=0, tiled=True),
        lax.all_to_all(grads_out, "grp", split_axis=0, concat_axis=0, tiled=True),
    )
    block_slots = lax.dynamic_slice_in_dim(
        token_slots, ep_index * grp_count * tok_dev, grp_count * tok_dev
    )
    to_here = (block_slots % grp_count == grp_index).astype(jnp.int32)
    source_place = (jnp.cumsum(to_here.reshape(grp_count, tok_dev), axis=1) - 1).reshape(-1)
    arrived_at = (
        jnp.repeat(jnp.arange(grp_count, dtype=jnp.int32), tok_dev) * row_cap + source_place
    )
    dest_cols = block_slots // grp_count
    col_onehot = (dest_cols[:, None] == jnp.arange(ep_count, dtype=jnp.int32)[None, :]).astype(
        jnp.int32
    ) * to_here[:, None]
    col_place = jnp.sum(jnp.cumsum(col_onehot, axis=0) * col_onehot, axis=1) - 1
    forward_place = jnp.where(to_here > 0, dest_cols * col_cap + col_place, ep_count * col_cap)
    mid_index = (
        jnp.full((ep_count * col_cap,), grp_count * row_cap, jnp.int32)
        .at[forward_place]
        .set(arrived_at, mode="drop")
    )
    inputs_fwd = padded_take(inputs_mid.reshape(-1, model_width), mid_index).reshape(
        ep_count, col_cap, model_width
    )
    grads_fwd = padded_take(grads_mid.reshape(-1, model_width), mid_index).reshape(
        ep_count, col_cap, model_width
    )
    inputs_slot, grads_slot = (
        lax.all_to_all(inputs_fwd, "ep", split_axis=0, concat_axis=0, tiled=True),
        lax.all_to_all(grads_fwd, "ep", split_axis=0, concat_axis=0, tiled=True),
    )
    my_slot = ep_index * grp_count + grp_index
    slot_hits = (token_slots == my_slot).astype(jnp.int32).reshape(ep_count, grp_count * tok_dev)
    arrivals = jnp.sum(slot_hits, axis=1)
    arrival_start = jnp.cumsum(arrivals) - arrivals
    capacity = slot_capacity.reshape(())
    within = jnp.arange(col_cap, dtype=jnp.int32)[None, :]
    slot_rank = arrival_start[:, None] + within
    kept_mask = (within < arrivals[:, None]) & (slot_rank < capacity)
    compact_place = jnp.where(kept_mask, slot_rank, cap_max).reshape(-1)
    compact_index = (
        jnp.full((cap_max,), ep_count * col_cap, jnp.int32)
        .at[compact_place]
        .set(jnp.arange(ep_count * col_cap, dtype=jnp.int32), mode="drop")
    )
    inputs_flat = inputs_slot.reshape(-1, model_width)
    grads_flat = grads_slot.reshape(-1, model_width)
    row_grads, grad_in, grad_out = slot_work(
        compact_index, inputs_flat, grads_flat, first_weight, second_weight
    )
    back_index = jnp.where(kept_mask, slot_rank, cap_max).reshape(-1)
    back_rows = padded_take(row_grads, back_index).reshape(ep_count, col_cap, model_width)
    mid_back = lax.all_to_all(back_rows, "ep", split_axis=0, concat_axis=0, tiled=True)
    return_place = jnp.where(to_here > 0, arrived_at, grp_count * row_cap)
    return_index = (
        jnp.full((grp_count * row_cap,), ep_count * col_cap, jnp.int32)
        .at[return_place]
        .set(forward_place, mode="drop")
    )
    source_back = padded_take(mid_back.reshape(-1, model_width), return_index).reshape(
        grp_count, row_cap, model_width
    )
    own_back = lax.all_to_all(source_back, "grp", split_axis=0, concat_axis=0, tiled=True)
    input_grads = own_back.reshape(-1, model_width)[send_place]
    owner_local = slot_experts.reshape(grp_count) - ep_index * EXP_COL
    member = (owner_local[:, None] == jnp.arange(EXP_COL, dtype=jnp.int32)[None, :]).astype(
        jnp.bfloat16
    )
    summed_list = []
    for slot_grad in (grad_in, grad_out):
        pieces = lax.all_to_all(
            slot_grad.reshape(grp_count, model_width // grp_count, hidden),
            "grp",
            split_axis=0,
            concat_axis=0,
            tiled=True,
        )
        summed = jnp.einsum("gk,gdf->kdf", member, pieces, preferred_element_type=jnp.float32)
        summed_list.append(summed.astype(jnp.bfloat16))
    expert_grads = jnp.stack(summed_list)
    return (input_grads, expert_grads)


def solution(mesh):
    in_specs = (
        P(("ep", "grp"), None),
        P(("ep", "grp"), None),
        P(("ep", "grp")),
        P(),
        P("ep", None),
        P("ep", "grp"),
        P("ep", "grp", None, None),
        P("ep", "grp", None, None),
    )
    out_specs = (P(("ep", "grp"), None), P(None, "ep", "grp", None))
    return jax.shard_map(
        per_device, mesh=mesh, in_specs=in_specs, out_specs=out_specs, check_vma=False
    )
```

profile of v0, /device:TPU:1, one launch (start us, length us, event | category | flops | bytes accessed | tf_op | source)
XLA Modules:
  0.0 286.4 jit_solution(10700731570833979834)
XLA Ops:
  6.5 16.7 %all-to-all-start.2 = ((bf16[24,8,768]{2,1,0:T(8,128)(2,1)}), bf16[24,8,768]{2,1,0:T(8,128)(2,1)S(1)}, u32[]{:S(2)}, u32[]{:S(2)}) async-start(bf16[24,8,768]{2,1,0:T(8,128)(2,1)} %bitcast.14), calls=%async_computation.2 | async-start | bytes 589824 | tf_op jit(solution)/shard_map/all_to_all | solution.py:87
  25.5 9.2 %reduce-window.18 = s32[32,24,128]{2,1,0:T(8,128)S(1)} reduce-window(s32[32,24,128]{2,1,0:T(8,128)S(1)} %fusion.37, s32[]{:T(128)} %constant.33.clone.1), window={size=1x1x128 pad=0_0x0_0x127_0}, to_apply=%region_3.4 | reduce-window | flops 12484608 | bytes 786436 | tf_op jit(solution)/shard_map/reduce-window
  35.5 3.6 %all-to-all-done.2 = bf16[24,8,768]{2,1,0:T(8,128)(2,1)S(1)} async-done(((bf16[24,8,768]{2,1,0:T(8,128)(2,1)}), bf16[24,8,768]{2,1,0:T(8,128)(2,1)S(1)}, u32[]{:S(2)}, u32[]{:S(2)}) %all-to-all-start.2) | async-done | bytes 294944 | tf_op jit(solution)/shard_map/all_to_all | solution.py:87
  39.1 6.1 %all-to-all-start = ((bf16[24,8,768]{2,1,0:T(8,128)(2,1)}), bf16[24,8,768]{2,1,0:T(8,128)(2,1)S(1)}, u32[]{:S(2)}, u32[]{:S(2)}) async-start(bf16[24,8,768]{2,1,0:T(8,128)(2,1)} %bitcast), calls=%async_computation | async-start | bytes 589824 | tf_op jit(solution)/shard_map/all_to_all | solution.py:88
  45.3 11.8 %scatter_custom_fusion.1 = s32[256]{0:T(256)S(1)} fusion(s32[3072]{0:T(1024)S(1)} %get-tuple-element.14, s32[3072]{0:T(1024)S(1)} %add_bitcast_fusion, s32[]{:T(128)} %constant.37.clone.1), kind=kCustom, calls=%fused_computation.90 | custom fusion | bytes 1028 | tf_op jit(solution)/shard_map/scatter | solution.py:107
  57.2 1.9 gather_fusion.4
  59.1 2.0 all-to-all-done
  61.1 9.7 %all-to-all-start.3 = ((bf16[32,8,768]{2,1,0:T(8,128)(2,1)}), bf16[32,8,768]{2,1,0:T(8,128)(2,1)S(1)}, u32[]{:S(2)}, u32[]{:S(2)}) async-start(bf16[32,8,768]{2,1,0:T(8,128)(2,1)} %bitcast.16), calls=%async_computation.3 | async-start | bytes 786432 | tf_op jit(solution)/shard_map/all_to_all | solution.py:116
  72.3 1.9 gather_fusion.1
  74.2 8.4 %all-to-all-done.3 = bf16[32,8,768]{2,1,0:T(8,128)(2,1)S(1)} async-done(((bf16[32,8,768]{2,1,0:T(8,128)(2,1)}), bf16[32,8,768]{2,1,0:T(8,128)(2,1)S(1)}, u32[]{:S(2)}, u32[]{:S(2)}) %all-to-all-start.3) | async-done | bytes 393248 | tf_op jit(solution)/shard_map/all_to_all | solution.py:116
  82.6 6.2 %all-to-all-start.1 = ((bf16[32,8,768]{2,1,0:T(8,128)(2,1)}), bf16[32,8,768]{2,1,0:T(8,128)(2,1)S(1)}, u32[]{:S(2)}, u32[]{:S(2)}) async-start(bf16[32,8,768]{2,1,0:T(8,128)(2,1)} %bitcast.8), calls=%async_computation.1 | async-start | bytes 786432 | tf_op jit(solution)/shard_map/all_to_all | solution.py:117
  90.5 10.2 %all-to-all-done.1 = bf16[32,8,768]{2,1,0:T(8,128)(2,1)S(1)} async-done(((bf16[32,8,768]{2,1,0:T(8,128)(2,1)}), bf16[32,8,768]{2,1,0:T(8,128)(2,1)S(1)}, u32[]{:S(2)}, u32[]{:S(2)}) %all-to-all-start.1) | async-done | bytes 393248 | tf_op jit(solution)/shard_map/all_to_all | solution.py:117
  107.2 1.9 gather_fusion.6
  109.2 6.0 %all-to-all-start.4 = ((bf16[32,8,768]{2,1,0:T(8,128)(2,1)}), bf16[32,8,768]{2,1,0:T(8,128)(2,1)S(1)}, u32[]{:S(2)}, u32[]{:S(2)}) async-start(bf16[32,8,768]{2,1,0:T(8,128)(2,1)} %bitcast.20), calls=%async_computation.4 | async-start | bytes 786432 | tf_op jit(solution)/shard_map/all_to_all | solution.py:140
  115.1 11.8 %scatter_custom_fusion.3 = s32[192]{0:T(256)S(1)} fusion(s32[3072]{0:T(1024)S(1)} %get-tuple-element.10, s32[3072]{0:T(1024)S(1)} %get-tuple-element.15, s32[]{:T(128)} %constant.45.clone.1), kind=kCustom, calls=%fused_computation.86 | custom fusion | bytes 772 | tf_op jit(solution)/shard_map/scatter | solution.py:145
  128.7 13.2 %all-to-all-start.5 = ((bf16[24,8,768]{2,1,0:T(8,128)(2,1)}), bf16[24,8,768]{2,1,0:T(8,128)(2,1)S(1)}, u32[]{:S(2)}, u32[]{:S(2)}) async-start(bf16[24,8,768]{2,1,0:T(8,128)(2,1)} %bitcast.22), calls=%async_computation.5 | async-start | bytes 589824 | tf_op jit(solution)/shard_map/all_to_all | solution.py:150
  142.0 2.9 %convolution_convert_fusion = bf16[768,1024]{1,0:T(8,128)(2,1)} fusion(bf16[256,768]{1,0:T(8,128)(2,1)} %copy-done.6, f32[256,1024]{1,0:T(8,128)S(1)} %copy-done.3), kind=kOutput, calls=%fused_computation.13 | convolution fusion | flops 405798912 | bytes 3014656 | tf_op jit(solution)/shard_map/dot_general | solution.py:43
  144.8 13.0 %all-to-all-done.5 = bf16[24,8,768]{2,1,0:T(8,128)(2,1)S(1)} async-done(((bf16[24,8,768]{2,1,0:T(8,128)(2,1)}), bf16[24,8,768]{2,1,0:T(8,128)(2,1)S(1)}, u32[]{:S(2)}, u32[]{:S(2)}) %all-to-all-start.5) | async-done | bytes 294944 | tf_op jit(solution)/shard_map/all_to_all | solution.py:150
  157.8 5.7 %all-to-all-start.7 = ((bf16[24,32,1024]{2,1,0:T(8,128)(2,1)}), bf16[24,32,1024]{2,1,0:T(8,128)(2,1)S(1)}, u32[]{:S(2)}, u32[]{:S(2)}) async-start(bf16[24,32,1024]{2,1,0:T(8,128)(2,1)} %bitcast.78), calls=%async_computation.7 | async-start | bytes 3145728 | tf_op jit(solution)/shard_map/all_to_all | solution.py:158
  163.6 2.9 %convolution_convert_fusion.1 = bf16[768,1024]{1,0:T(8,128)(2,1)} fusion(bf16[256,768]{1,0:T(8,128)(2,1)} %copy-done.1, bf16[256,1024]{1,0:T(8,128)(2,1)} %copy-done.4), kind=kOutput, calls=%fused_computation.14 | convolution fusion | flops 403439616 | bytes 2490368 | tf_op jit(solution)/shard_map/dot_general | solution.py:40
  166.5 53.5 %all-to-all-done.7 = bf16[24,32,1024]{2,1,0:T(8,128)(2,1)S(1)} async-done(((bf16[24,32,1024]{2,1,0:T(8,128)(2,1)}), bf16[24,32,1024]{2,1,0:T(8,128)(2,1)S(1)}, u32[]{:S(2)}, u32[]{:S(2)}) %all-to-all-start.7) | async-done | bytes 1572896 | tf_op jit(solution)/shard_map/all_to_all | solution.py:158
  220.0 6.0 %all-to-all-start.6 = ((bf16[24,32,1024]{2,1,0:T(8,128)(2,1)}), bf16[24,32,1024]{2,1,0:T(8,128)(2,1)}, u32[]{:S(2)}, u32[]{:S(2)}) async-start(bf16[24,32,1024]{2,1,0:T(8,128)(2,1)} %bitcast.77), calls=%async_computation.6 | async-start | bytes 3145728 | tf_op jit(solution)/shard_map/all_to_all | solution.py:158
  228.7 53.8 %all-to-all-done.6 = bf16[24,32,1024]{2,1,0:T(8,128)(2,1)} async-done(((bf16[24,32,1024]{2,1,0:T(8,128)(2,1)}), bf16[24,32,1024]{2,1,0:T(8,128)(2,1)}, u32[]{:S(2)}, u32[]{:S(2)}) %all-to-all-start.6) | async-done | bytes 1572896 | tf_op jit(solution)/shard_map/all_to_all | solution.py:158
  282.5 2.6 fusion.28
  (89 shorter events, 23.7 us)
Async XLA Ops:
  0.6 102.6 %copy-start = (bf16[1,1,768,1024]{3,2,1,0:T(8,128)(2,1)S(1)}, bf16[1,1,768,1024]{3,2,1,0:T(8,128)(2,1)}, u32[]{:S(2)}) copy-start(bf16[1,1,768,1024]{3,2,1,0:T(8,128)(2,1)} %param.14) | copy-start | bytes 4718596
  4.7 18.5 %copy-start.7 = (bf16[128,768]{1,0:T(8,128)(2,1)S(1)}, bf16[128,768]{1,0:T(8,128)(2,1)}, u32[]{:S(2)}) copy-start(bf16[128,768]{1,0:T(8,128)(2,1)} %param.9) | copy-start | bytes 589828
  4.7 18.5 %copy-start.8 = (f32[128]{0:T(128)S(1)}, f32[128]{0:T(128)}, u32[]{:S(2)}) copy-start(f32[128]{0:T(128)} %param.10) | copy-start | bytes 1540
  4.8 18.6 %copy-start.5 = (s32[98304]{0:T(1024)S(1)}, s32[98304]{0:T(1024)}, u32[]{:S(2)}) copy-start(s32[98304]{0:T(1024)} %param.11) | copy-start | bytes 1179652
  6.5 32.6 %all-to-all-start.2 = ((bf16[24,8,768]{2,1,0:T(8,128)(2,1)}), bf16[24,8,768]{2,1,0:T(8,128)(2,1)S(1)}, u32[]{:S(2)}, u32[]{:S(2)}) async-start(bf16[24,8,768]{2,1,0:T(8,128)(2,1)} %bitcast.14), calls=%async_computation.2 | async-start | bytes 589824 | tf_op jit(solution)/shard_map/all_to_all | solution.py:87
  39.1 22.0 %all-to-all-start = ((bf16[24,8,768]{2,1,0:T(8,128)(2,1)}), bf16[24,8,768]{2,1,0:T(8,128)(2,1)S(1)}, u32[]{:S(2)}, u32[]{:S(2)}) async-start(bf16[24,8,768]{2,1,0:T(8,128)(2,1)} %bitcast), calls=%async_computation | async-start | bytes 589824 | tf_op jit(solution)/shard_map/all_to_all | solution.py:88
  61.1 21.5 %all-to-all-start.3 = ((bf16[32,8,768]{2,1,0:T(8,128)(2,1)}), bf16[32,8,768]{2,1,0:T(8,128)(2,1)S(1)}, u32[]{:S(2)}, u32[]{:S(2)}) async-start(bf16[32,8,768]{2,1,0:T(8,128)(2,1)} %bitcast.16), calls=%async_computation.3 | async-start | bytes 786432 | tf_op jit(solution)/shard_map/all_to_all | solution.py:116
  82.6 18.2 %all-to-all-start.1 = ((bf16[32,8,768]{2,1,0:T(8,128)(2,1)}), bf16[32,8,768]{2,1,0:T(8,128)(2,1)S(1)}, u32[]{:S(2)}, u32[]{:S(2)}) async-start(bf16[32,8,768]{2,1,0:T(8,128)(2,1)} %bitcast.8), calls=%async_computation.1 | async-start | bytes 786432 | tf_op jit(solution)/shard_map/all_to_all | solution.py:117
  102.0 1.2 copy-start.1
  103.2 2.6 copy-start.6
  103.2 1.6 copy-start.9
  103.8 1.0 copy-start.2
  105.8 0.8 copy-start.4
  109.2 17.8 %all-to-all-start.4 = ((bf16[32,8,768]{2,1,0:T(8,128)(2,1)}), bf16[32,8,768]{2,1,0:T(8,128)(2,1)S(1)}, u32[]{:S(2)}, u32[]{:S(2)}) async-start(bf16[32,8,768]{2,1,0:T(8,128)(2,1)} %bitcast.20), calls=%async_computation.4 | async-start | bytes 786432 | tf_op jit(solution)/shard_map/all_to_all | solution.py:140
  127.0 15.0 %copy-start.3 = (f32[256,1024]{1,0:T(8,128)S(1)}, f32[256,1024]{1,0:T(8,128)}, u32[]{:S(2)}) copy-start(f32[256,1024]{1,0:T(8,128)} %copy-done.2) | copy-start | bytes 3145732
  128.7 29.1 %all-to-all-start.5 = ((bf16[24,8,768]{2,1,0:T(8,128)(2,1)}), bf16[24,8,768]{2,1,0:T(8,128)(2,1)S(1)}, u32[]{:S(2)}, u32[]{:S(2)}) async-start(bf16[24,8,768]{2,1,0:T(8,128)(2,1)} %bitcast.22), calls=%async_computation.5 | async-start | bytes 589824 | tf_op jit(solution)/shard_map/all_to_all | solution.py:150
  157.8 62.2 %all-to-all-start.7 = ((bf16[24,32,1024]{2,1,0:T(8,128)(2,1)}), bf16[24,32,1024]{2,1,0:T(8,128)(2,1)S(1)}, u32[]{:S(2)}, u32[]{:S(2)}) async-start(bf16[24,32,1024]{2,1,0:T(8,128)(2,1)} %bitcast.78), calls=%async_computation.7 | async-start | bytes 3145728 | tf_op jit(solution)/shard_map/all_to_all | solution.py:158
  220.0 6.0 %copy-start.10 = (s32[1,24]{1,0:T(1,128)S(1)}, s32[1,24]{1,0:T(1,128)}, u32[]{:S(2)}) copy-start(s32[1,24]{1,0:T(1,128)} %param.12) | copy-start | bytes 292
  220.0 62.5 %all-to-all-start.6 = ((bf16[24,32,1024]{2,1,0:T(8,128)(2,1)}), bf16[24,32,1024]{2,1,0:T(8,128)(2,1)}, u32[]{:S(2)}, u32[]{:S(2)}) async-start(bf16[24,32,1024]{2,1,0:T(8,128)(2,1)} %bitcast.77), calls=%async_computation.6 | async-start | bytes 3145728 | tf_op jit(solution)/shard_map/all_to_all | solution.py:158
where the time goes:
time: 287 us; the launch traced here: 286 us
  waiting for transfers between devices  144 us (50%)
  starting transfers between devices  69.5 us (24%)
  local copies, waits for them, and re-layouts  45.7 us (16%)
  other arithmetic  13.2 us (5%)
  matrix products  11.7 us (4%)
    all_to_all x2, waiting for transfers between devices, per_device(): lax.all_to_all(slot_grad.reshape(grp_count, model_width // grp_count, hid...  107 us
    all_to_all x1, starting transfers between devices, per_device(): lax.all_to_all(inputs_out, 'grp', split_axis=0, concat_axis=0, tiled=True)  16.7 us
    gather x8, local copies, waits for them, and re-layouts, padded_take(): return jnp.concatenate([source, filler], axis=0)[take_index]  13.4 us
    all_to_all x1, starting transfers between devices, per_device(): lax.all_to_all(source_back, 'grp', split_axis=0, concat_axis=0, tiled=True)  13.2 us
    all_to_all x1, waiting for transfers between devices, per_device(): lax.all_to_all(source_back, 'grp', split_axis=0, concat_axis=0, tiled=True)  13 us
    scatter x1, local copies, waits for them, and re-layouts, per_device(): return_index = jnp.full((grp_count * row_cap,), ep_count * col_cap, jnp.i...  11.8 us
    scatter x1, local copies, waits for them, and re-layouts, per_device(): mid_index = jnp.full((ep_count * col_cap,), grp_count * row_cap, jnp.int3...  11.8 us
    all_to_all x2, starting transfers between devices, per_device(): lax.all_to_all(slot_grad.reshape(grp_count, model_width // grp_count, hid...  11.7 us
  transfers between devices with their start and end apart: 8, of which 7 were waited for; matrix products, arithmetic and copies ran while one was open for 18% of the time, Pallas kernels for 0%

commit v1 on v0

v1 whole, which is shorter than its diff:
```python
import jax
import jax.numpy as jnp
from jax import lax
from jax.experimental import pallas as pl
from jax.experimental.pallas import tpu as pltpu
from jax.sharding import PartitionSpec as P

EP = 32
GRP = 24
Z = 12
EXP_COL = 4
TOK = 128
CAP = 8
D = 768
FF = 1024
ROWS_MID = GRP * CAP
ROWS_SLOT = EP * CAP
FEAT = D // GRP

coef_a = 0.7978845608028654
coef_b = 0.044715

f32 = jnp.float32
bf16 = jnp.bfloat16
i32 = jnp.int32


def iota(shape, dim):
    return lax.broadcasted_iota(i32, shape, dim)


def split_slot(slots):
    col = (slots * 2731) >> 16
    return col, slots - col * GRP


def to_column(row):
    n = row.shape[1]
    eye = iota((n, n), 0) == iota((n, n), 1)
    return jnp.sum(jnp.where(eye, jnp.broadcast_to(row, (n, n)), 0.0), axis=1, keepdims=True)


def to_row(column):
    n = column.shape[0]
    eye = iota((n, n), 0) == iota((n, n), 1)
    return jnp.sum(jnp.where(eye, jnp.broadcast_to(column, (n, n)), 0.0), axis=0, keepdims=True)


def earlier_equal(row):
    n = row.shape[1]
    same = to_column(row) == row
    before = iota((n, n), 0) < iota((n, n), 1)
    return jnp.sum(jnp.where(same & before, 1.0, 0.0), axis=0, keepdims=True)


def send_kernel(place_ref, slots_ref, inputs_ref, grads_ref, gate_ref, rows_ref, pick_ref):
    own = place_ref[0] * GRP + place_ref[1]
    slots = slots_ref[pl.ds(own % 8, 1), :]
    dest = split_slot(slots)[1].astype(f32)
    spot = dest * CAP + earlier_equal(dest)
    pick = (iota((ROWS_MID, TOK), 0).astype(f32) == spot).astype(bf16)
    pick_ref[...] = pick
    scaled = (to_column(gate_ref[...]) * grads_ref[...].astype(f32)).astype(bf16)
    rows_ref[:, :D] = jnp.dot(pick, inputs_ref[...], preferred_element_type=f32).astype(bf16)
    rows_ref[:, D:] = jnp.dot(pick, scaled, preferred_element_type=f32).astype(bf16)


def route_kernel(place_ref, block_ref, slots_ref, capacity_ref, forward_ref, kept_ref, wide_ref):
    grp_index = place_ref[1]
    col, row = split_slot(block_ref[...])
    hit = jnp.where(row == grp_index, 1.0, 0.0)
    upper = (iota((TOK, TOK), 0) < iota((TOK, TOK), 1)).astype(bf16)
    spot = jnp.dot(hit.astype(bf16), upper, preferred_element_type=f32)
    value = hit * (col + 1).astype(f32)
    lane = iota((CAP, TOK), 0).astype(f32)
    for s in range(GRP):
        wide_ref[s * CAP : (s + 1) * CAP, :] = jnp.where(
            spot[s : s + 1, :] == lane, jnp.broadcast_to(value[s : s + 1, :], (CAP, TOK)), 0.0
        )
    dest = to_row(jnp.sum(wide_ref[...], axis=1, keepdims=True))
    target = jnp.where(dest > 0.0, (dest - 1.0) * CAP + earlier_equal(dest), -1.0)
    forward_ref[...] = (iota((ROWS_SLOT, ROWS_MID), 0).astype(f32) == target).astype(bf16)
    my_slot = place_ref[0] * GRP + grp_index
    arrived = jnp.concatenate(
        [
            jnp.sum(
                jnp.where(slots_ref[e * GRP : (e + 1) * GRP, :] == my_slot, 1.0, 0.0),
                axis=0,
                keepdims=True,
            )
            for e in range(EP)
        ],
        axis=0,
    ).astype(bf16)
    counts = jnp.dot(arrived, jnp.ones((TOK, TOK), bf16), preferred_element_type=f32)
    lower = (iota((EP, EP), 1) < iota((EP, EP), 0)).astype(bf16)
    starts = jnp.dot(lower, counts.astype(bf16), preferred_element_type=f32)
    capacity = capacity_ref[0].astype(f32)
    for e in range(EP):
        kept = (lane < counts[e : e + 1, :]) & (starts[e : e + 1, :] + lane < capacity)
        kept_ref[e * CAP : (e + 1) * CAP, :] = jnp.where(kept, 1.0, 0.0)


def forward_kernel(forward_ref, rows_ref, out_ref):
    out_ref[...] = jnp.dot(forward_ref[...], rows_ref[...], preferred_element_type=f32).astype(bf16)


def back_kernel(pick_ref, rows_ref, out_ref):
    out_ref[...] = lax.dot_general(
        pick_ref[...], rows_ref[...], (((0,), (0,)), ((), ())), preferred_element_type=f32
    ).astype(bf16)


def gelu_pair(preact):
    square = preact * preact
    tanh_value = jnp.tanh(coef_a * preact * (1.0 + coef_b * square))
    half_sum = 0.5 * (1.0 + tanh_value)
    gelu_value = preact * half_sum
    gelu_slope = half_sum + 0.5 * preact * (1.0 - tanh_value * tanh_value) * coef_a * (
        1.0 + 3.0 * coef_b * square
    )
    return gelu_value, gelu_slope


def slot_kernel(
    place_ref, rows_ref, kept_ref, first_ref, second_ref, back_ref, mine_ref, other_ref, grad_ref
):
    core = place_ref[1] % 2
    kept = kept_ref[:, 0:1] > 0.0
    inputs = jnp.where(kept, rows_ref[:, :D].astype(f32), 0.0).astype(bf16)
    grads = jnp.where(kept, rows_ref[:, D:].astype(f32), 0.0).astype(bf16)
    preact = jnp.dot(inputs, first_ref[...], preferred_element_type=f32)
    hidden_grad = jnp.dot(grads, second_ref[...], preferred_element_type=f32)
    gelu_value, gelu_slope = gelu_pair(preact)
    activated = gelu_value.astype(bf16)
    preact_grad = (hidden_grad * gelu_slope).astype(bf16)
    for k, (left, right) in enumerate(((inputs, preact_grad), (grads, activated))):
        grad_ref[...] = lax.dot_general(
            left, right, (((0,), (0,)), ((), ())), preferred_element_type=f32
        ).astype(bf16)
        for z in range(Z):
            start = z * 2 * FEAT
            mine = pl.multiple_of(start + core * FEAT, FEAT)
            other = pl.multiple_of(start + (1 - core) * FEAT, FEAT)
            mine_ref[z, k] = grad_ref[pl.ds(mine, FEAT), :]
            other_ref[z, k] = grad_ref[pl.ds(other, FEAT), :]
    back_ref[...] = lax.dot_general(
        preact_grad, first_ref[...], (((1,), (1,)), ((), ())), preferred_element_type=f32
    ).astype(bf16)


def merge_kernel(owner_ref, mine_ref, partner_ref, out_ref):
    for k in range(2):
        mine = mine_ref[0, k].astype(f32)
        partner = partner_ref[0, k].astype(f32)
        for e in range(EXP_COL):
            first = jnp.where(owner_ref[0] == e, mine, 0.0)
            second = jnp.where(owner_ref[1] == e, partner, 0.0)
            out_ref[0, k, e] = (first + second).astype(bf16)


def shape(dims, dtype=bf16):
    return jax.ShapeDtypeStruct(dims, dtype)


def whole():
    return pl.BlockSpec(memory_space=pltpu.VMEM)


def scalars():
    return pl.BlockSpec(memory_space=pltpu.SMEM)


def per_device(
    token_inputs,
    output_grads,
    gate_probs,
    token_slots,
    slot_experts,
    slot_capacity,
    weight_in,
    weight_out,
):
    ep_index = lax.axis_index("ep")
    grp_index = lax.axis_index("grp")
    place = jnp.stack([ep_index, grp_index]).astype(i32)
    slots = token_slots.reshape(EP * GRP, TOK)

    rows_out, pick = pl.pallas_call(
        send_kernel,
        grid_spec=pltpu.PrefetchScalarGridSpec(
            num_scalar_prefetch=1,
            grid=(1,),
            in_specs=[
                pl.BlockSpec((8, TOK), lambda i, p: ((p[0] * GRP + p[1]) // 8, 0)),
                pl.BlockSpec((TOK, D), lambda i, p: (0, 0)),
                pl.BlockSpec((TOK, D), lambda i, p: (0, 0)),
                pl.BlockSpec((1, TOK), lambda i, p: (0, 0)),
            ],
            out_specs=[
                pl.BlockSpec((ROWS_MID, 2 * D), lambda i, p: (0, 0)),
                pl.BlockSpec((ROWS_MID, TOK), lambda i, p: (0, 0)),
            ],
        ),
        out_shape=[shape((ROWS_MID, 2 * D)), shape((ROWS_MID, TOK))],
        name="send",
    )(place, slots, token_inputs, output_grads, gate_probs.reshape(1, TOK))
    rows_mid = lax.all_to_all(
        rows_out.reshape(GRP, CAP, 2 * D), "grp", split_axis=0, concat_axis=0, tiled=True
    ).reshape(ROWS_MID, 2 * D)

    forward, kept = pl.pallas_call(
        route_kernel,
        grid_spec=pltpu.PrefetchScalarGridSpec(
            num_scalar_prefetch=1,
            grid=(1,),
            in_specs=[
                pl.BlockSpec((GRP, TOK), lambda i, p: (p[0], 0)),
                pl.BlockSpec((EP * GRP, TOK), lambda i, p: (0, 0)),
                pl.BlockSpec(memory_space=pltpu.SMEM),
            ],
            out_specs=[
                pl.BlockSpec((ROWS_SLOT, ROWS_MID), lambda i, p: (0, 0)),
                pl.BlockSpec((ROWS_SLOT, TOK), lambda i, p: (0, 0)),
            ],
            scratch_shapes=[pltpu.VMEM((ROWS_MID, TOK), f32)],
        ),
        out_shape=[shape((ROWS_SLOT, ROWS_MID)), shape((ROWS_SLOT, TOK), f32)],
        name="route",
    )(place, slots, slots, slot_capacity.reshape(1))

    rows_fwd = pl.pallas_call(
        forward_kernel,
        in_specs=[whole(), whole()],
        out_specs=whole(),
        out_shape=shape((ROWS_SLOT, 2 * D)),
        name="forward",
    )(forward, rows_mid)
    rows_slot = lax.all_to_all(
        rows_fwd.reshape(EP, CAP, 2 * D), "ep", split_axis=0, concat_axis=0, tiled=True
    ).reshape(ROWS_SLOT, 2 * D)

    back_rows, mine, other = pl.pallas_call(
        slot_kernel,
        in_specs=[scalars()] + [whole()] * 4,
        out_specs=[whole()] * 3,
        out_shape=[
            shape((ROWS_SLOT, D)),
            shape((Z, 2, FEAT, FF)),
            shape((Z, 2, FEAT, FF)),
        ],
        scratch_shapes=[pltpu.VMEM((D, FF), bf16)],
        name="slot",
    )(place, rows_slot, kept, weight_in.reshape(D, FF), weight_out.reshape(D, FF))

    partner = lax.ppermute(other, "grp", [(g, g ^ 1) for g in range(GRP)])
    experts = slot_experts.reshape(GRP) - ep_index * EXP_COL
    owners = lax.dynamic_slice_in_dim(experts, (grp_index // 2) * 2, 2)
    owners = jnp.where(grp_index % 2 == 0, owners, owners[::-1])
    merged = pl.pallas_call(
        merge_kernel,
        grid_spec=pltpu.PrefetchScalarGridSpec(
            num_scalar_prefetch=1,
            grid=(Z,),
            in_specs=[pl.BlockSpec((1, 2, FEAT, FF), lambda i, p: (i, 0, 0, 0))] * 2,
            out_specs=pl.BlockSpec((1, 2, EXP_COL, FEAT, FF), lambda i, p: (i, 0, 0, 0, 0)),
        ),
        out_shape=shape((Z, 2, EXP_COL, FEAT, FF)),
        name="merge",
    )(owners, mine, partner)
    expert_grads = lax.psum_scatter(
        merged.reshape(Z * 2 * EXP_COL * FEAT, FF),
        "grp",
        scatter_dimension=0,
        tiled=True,
        axis_index_groups=[[2 * z + c for z in range(Z)] for c in range(2)],
    ).reshape(2, EXP_COL, FEAT, FF)

    mid_back = lax.all_to_all(
        back_rows.reshape(EP, CAP, D), "ep", split_axis=0, concat_axis=0, tiled=True
    ).reshape(ROWS_SLOT, D)
    source_back = pl.pallas_call(
        back_kernel,
        in_specs=[whole(), whole()],
        out_specs=whole(),
        out_shape=shape((ROWS_MID, D)),
        name="back_mid",
    )(forward, mid_back)
    own_back = lax.all_to_all(
        source_back.reshape(GRP, CAP, D), "grp", split_axis=0, concat_axis=0, tiled=True
    ).reshape(ROWS_MID, D)
    input_grads = pl.pallas_call(
        back_kernel,
        in_specs=[whole(), whole()],
        out_specs=whole(),
        out_shape=shape((TOK, D)),
        name="back_own",
    )(pick, own_back)
    return input_grads, expert_grads


def solution(mesh):
    in_specs = (
        P(("ep", "grp"), None),
        P(("ep", "grp"), None),
        P(("ep", "grp")),
        P(),
        P("ep", None),
        P("ep", "grp"),
        P("ep", "grp", None, None),
        P("ep", "grp", None, None),
    )
    out_specs = (P(("ep", "grp"), None), P(None, "ep", "grp", None))
    return jax.shard_map(
        per_device, mesh=mesh, in_specs=in_specs, out_specs=out_specs, check_vma=False
    )
```

time: 287 us -> 206 us (0.72)
  waiting for transfers between devices: 144 us -> 59 us
  blocking collectives: 0 us -> 75 us
  starting transfers between devices: 69.5 us -> 23.1 us
  local copies, waits for them, and re-layouts: 45.7 us -> 3.23 us
  Pallas kernels: 0 us -> 29.1 us
  between operations: 1.87 us -> 14.8 us
  other arithmetic: 13.2 us -> 1.26 us
  matrix products: 11.7 us -> 0 us
    all_to_all x8 -> x1, waiting for transfers between devices: 144 us -> 21.4 us  [per_device(): lax.all_to_all(rows_out.reshape(GRP, CAP, 2 * D), 'grp', split_axis=0, co...]
    all_to_all x0 -> x3, blocking collectives: none -> 75 us  [the longest x1 29.5 us: per_device(): lax.all_to_all(rows_fwd.reshape(EP, CAP, 2 * D), 'ep', split_axis=0, conc...]
    all_to_all x8 -> x1, starting transfers between devices: 69.5 us -> 16.7 us  [per_device(): lax.all_to_all(rows_out.reshape(GRP, CAP, 2 * D), 'grp', split_axis=0, co...]
    reduce_scatter x0 -> x1, waiting for transfers between devices: none -> 35.2 us  [per_device(): lax.psum_scatter(merged.reshape(Z * 2 * EXP_COL * FEAT, FF), 'grp', scatt...]
    pallas_call x0 -> x7, Pallas kernels: none -> 29.1 us  [the longest x1 9.98 us: per_device(): pl.pallas_call(merge_kernel, grid_spec=pltpu.PrefetchScalarGridSpec(num_s...]
    scatter x4 -> x0, local copies, waits for them, and re-layouts: 26.1 us -> none  [the longest x1 11.8 us: per_device(): return_index = jnp.full((grp_count * row_cap,), ep_count * col_cap, jnp.i...]
    gather x9 -> x0, local copies, waits for them, and re-layouts: 14.9 us -> none  [the longest x8 13.4 us: padded_take(): return jnp.concatenate([source, filler], axis=0)[take_index]]
    dot_general x7 -> x0, matrix products: 11.7 us -> none  [the longest x2 3.76 us: per_device(): jnp.einsum('gk,gdf->kdf', member, pieces, preferred_element_type=jnp.floa...]
  transfers between devices with their start and end apart: 8 -> 3, of which waited for: 7 -> 3; matrix products, arithmetic and copies ran while one was open for 18% -> 0% of each run, Pallas kernels for 0% -> 3%
where the time goes in v1:
time: 206 us; the launch traced here: 205 us
  blocking collectives  75 us (36%)
  waiting for transfers between devices  59 us (29%)
  Pallas kernels  29.1 us (14%)
  starting transfers between devices  23.1 us (11%)
  between operations  14.8 us (7%)
  local copies, waits for them, and re-layouts  3.23 us (2%)
    reduce_scatter x1, waiting for transfers between devices, per_device(): lax.psum_scatter(merged.reshape(Z * 2 * EXP_COL * FEAT, FF), 'grp', scatt...  35.2 us
    all_to_all x1, blocking collectives, per_device(): lax.all_to_all(rows_fwd.reshape(EP, CAP, 2 * D), 'ep', split_axis=0, conc...  29.5 us
    all_to_all x1, blocking collectives, per_device(): lax.all_to_all(source_back.reshape(GRP, CAP, D), 'grp', split_axis=0, con...  27.2 us
    all_to_all x1, waiting for transfers between devices, per_device(): lax.all_to_all(rows_out.reshape(GRP, CAP, 2 * D), 'grp', split_axis=0, co...  21.4 us
    all_to_all x1, blocking collectives, per_device(): lax.all_to_all(back_rows.reshape(EP, CAP, D), 'ep', split_axis=0, concat_...  18.3 us
    all_to_all x1, starting transfers between devices, per_device(): lax.all_to_all(rows_out.reshape(GRP, CAP, 2 * D), 'grp', split_axis=0, co...  16.7 us
    pallas_call x1, Pallas kernels, per_device(): pl.pallas_call(merge_kernel, grid_spec=pltpu.PrefetchScalarGridSpec(num_s...  9.98 us
    pallas_call x1, Pallas kernels, per_device(): pl.pallas_call(slot_kernel, in_specs=[scalars()] + [whole()] * 4, out_spe...  7.13 us
  transfers between devices with their start and end apart: 3, of which 3 were waited for; matrix products, arithmetic and copies ran while one was open for 0% of the time, Pallas kernels for 3%

profile of v1, /device:TPU:1, one launch (start us, length us, event | category | flops | bytes accessed | tf_op | source)
XLA Modules:
  0.0 205.4 jit_solution(10885704914548455856)
XLA Ops:
  7.2 0.7 pad_add_fusion.place_ref
  7.8 2.9 %send.1 = (bf16[192,1536]{1,0:T(8,128)(2,1)}, bf16[192,128]{1,0:T(8,128)(2,1)}) custom-call(s32[2]{0:T(128)} %pad_add_fusion.place_ref, s32[768,128]{1,0:T(8,128)} %bitcast.23, bf16[128,768]{1,0:T(8,128)(2,1)} %inputs_ref.1, bf16[128,768]{1,0:T(8,128)(2,1)} %grads_ref.1, f32[1,128]{1,0:T(1,128)} %bitcast.36), custom_call_target="tpu_custom_call" | custom-call | tf_op jit(solution)/shard_map/send/pallas_call | solution.py:189
  10.7 16.7 %all-to-all-start = ((bf16[24,8,1536]{2,1,0:T(8,128)(2,1)}), bf16[24,8,1536]{2,1,0:T(8,128)(2,1)S(1)}, u32[]{:S(2)}, u32[]{:S(2)}) async-start(bf16[24,8,1536]{2,1,0:T(8,128)(2,1)} %bitcast.34), calls=%async_computation | async-start | bytes 1179648 | tf_op jit(solution)/shard_map/all_to_all | solution.py:208
  27.4 0.0 reduce-scatter.2.cloned.1.call-start
  28.1 2.8 %route.1 = (bf16[256,192]{1,0:T(8,128)(2,1)}, f32[256,128]{1,0:T(8,128)}) custom-call(s32[2]{0:T(128)} %pad_add_fusion.place_ref, s32[768,128]{1,0:T(8,128)} %bitcast.24, s32[768,128]{1,0:T(8,128)} %bitcast.25, s32[1]{0:T(128)} %bitcast.21.capacity_ref), custom_call_target="tpu_custom_call" | custom-call | tf_op jit(solution)/shard_map/route/pallas_call | solution.py:212
  30.9 21.4 %all-to-all-done = bf16[24,8,1536]{2,1,0:T(8,128)(2,1)S(1)} async-done(((bf16[24,8,1536]{2,1,0:T(8,128)(2,1)}), bf16[24,8,1536]{2,1,0:T(8,128)(2,1)S(1)}, u32[]{:S(2)}, u32[]{:S(2)}) %all-to-all-start) | async-done | bytes 589856 | tf_op jit(solution)/shard_map/all_to_all | solution.py:208
  52.3 0.8 copy-done
  53.1 2.4 %forward.1 = bf16[256,1536]{1,0:T(8,128)(2,1)} custom-call(bf16[256,192]{1,0:T(8,128)(2,1)} %get-tuple-element.10.forward_ref.pick_ref, bf16[192,1536]{1,0:T(8,128)(2,1)} %bitcast.28), custom_call_target="tpu_custom_call" | custom-call | tf_op jit(solution)/shard_map/forward/pallas_call | solution.py:232
  55.5 29.5 %all_to_all.20 = bf16[32,8,1536]{2,1,0:T(8,128)(2,1)} all-to-all(bf16[32,8,1536]{2,1,0:T(8,128)(2,1)} %bitcast.27), channel_id=1, replica_groups=mesh['ep'=32,'grp'=24] {'ep'}, dimensions={0} | all-to-all | bytes 1572864 | tf_op jit(solution)/shard_map/all_to_all | solution.py:239
  85.0 7.1 %slot.1 = (bf16[256,768]{1,0:T(8,128)(2,1)}, bf16[12,2,32,1024]{3,2,1,0:T(8,128)(2,1)}, bf16[12,2,32,1024]{3,2,1,0:T(8,128)(2,1)}) custom-call(s32[2]{0:T(128)} %pad_add_fusion.place_ref, bf16[256,1536]{1,0:T(8,128)(2,1)} %bitcast.26, f32[256,128]{1,0:T(8,128)} %get-tuple-element.12.kept_ref, bf16[768,1024]{1,0:T(8,128)(2,1)} %bitcast.29, ...), custom_call_target="tpu_custom_call" | custom-call | tf_op jit(solution)/shard_map/slot/pallas_call | solution.py:243
  92.1 6.3 %collective-permute-start = (bf16[12,2,32,1024]{3,2,1,0:T(8,128)(2,1)}, bf16[12,2,32,1024]{3,2,1,0:T(8,128)(2,1)S(1)}, u32[]{:S(2)}, u32[]{:S(2)}) collective-permute-start(bf16[12,2,32,1024]{3,2,1,0:T(8,128)(2,1)} %get-tuple-element.15), channel_id=1, source_target_pairs={{0,1},{1,0},{2,3},{3,2},{4,5},{5,4},{6,7},{7,6},{8,9},{9,8},{10,11... | collective-permute-start | bytes 4718600 | tf_op jit(solution)/shard_map/ppermute | solution.py:256
  98.5 0.1 dynamic-slice_bitcast_fusion
  98.6 0.1 rev.3
  98.7 0.6 broadcast_select_fusion.owner_ref
  99.3 2.4 %collective-permute-done.partner_ref = bf16[12,2,32,1024]{3,2,1,0:T(8,128)(2,1)S(1)} collective-permute-done((bf16[12,2,32,1024]{3,2,1,0:T(8,128)(2,1)}, bf16[12,2,32,1024]{3,2,1,0:T(8,128)(2,1)S(1)}, u32[]{:S(2)}, u32[]{:S(2)}) %collective-permute-start) | collective-permute-done | bytes 1572896 | tf_op jit(solution)/shard_map/ppermute | solution.py:256
  101.7 1.2 copy-done.1
  102.9 10.0 %merge.1 = bf16[12,2,4,32,1024]{4,3,2,1,0:T(8,128)(2,1)} custom-call(s32[2]{0:T(128)} %broadcast_select_fusion.owner_ref, bf16[12,2,32,1024]{3,2,1,0:T(8,128)(2,1)} %get-tuple-element.14.mine_ref, bf16[12,2,32,1024]{3,2,1,0:T(8,128)(2,1)} %copy-done.1), custom_call_target="tpu_custom_call" | custom-call | tf_op jit(solution)/shard_map/merge/pallas_call | solution.py:260
  112.9 0.0 reduce-scatter.2.cloned.1.call-update
  112.9 1.0 copy-done.2
  113.9 18.3 %all_to_all.21 = bf16[32,8,768]{2,1,0:T(8,128)(2,1)} all-to-all(bf16[32,8,768]{2,1,0:T(8,128)(2,1)S(1)} %bitcast.35), channel_id=1, replica_groups=mesh['ep'=32,'grp'=24] {'ep'}, dimensions={0} | all-to-all | bytes 786432 | tf_op jit(solution)/shard_map/all_to_all | solution.py:279
  132.2 2.1 %back_mid.1 = bf16[192,768]{1,0:T(8,128)(2,1)} custom-call(bf16[256,192]{1,0:T(8,128)(2,1)} %get-tuple-element.10.forward_ref.pick_ref, bf16[256,768]{1,0:T(8,128)(2,1)} %bitcast.31), custom_call_target="tpu_custom_call" | custom-call | tf_op jit(solution)/shard_map/back_mid/pallas_call | solution.py:282
  134.3 27.2 %all_to_all.22 = bf16[24,8,768]{2,1,0:T(8,128)(2,1)} all-to-all(bf16[24,8,768]{2,1,0:T(8,128)(2,1)} %bitcast.32), channel_id=1, replica_groups=mesh['ep'=32,'grp'=24] {'grp'}, dimensions={0} | all-to-all | bytes 589824 | tf_op jit(solution)/shard_map/all_to_all | solution.py:289
  161.5 1.9 back_own.1
  163.4 35.2 %reduce-scatter.2.cloned.1.call-done = bf16[256,1024]{1,0:T(8,128)(2,1)} async-done(((bf16[3072,1024]{1,0:T(8,128)(2,1)}), bf16[256,1024]{1,0:T(8,128)(2,1)}) %reduce-scatter.2.cloned.1.call-update) | async-done | bytes 524304 | tf_op jit(solution)/shard_map/reduce_scatter | solution.py:271
  (6 shorter events, 0.0 us)
Async XLA Ops:
  10.7 41.5 %all-to-all-start = ((bf16[24,8,1536]{2,1,0:T(8,128)(2,1)}), bf16[24,8,1536]{2,1,0:T(8,128)(2,1)S(1)}, u32[]{:S(2)}, u32[]{:S(2)}) async-start(bf16[24,8,1536]{2,1,0:T(8,128)(2,1)} %bitcast.34), calls=%async_computation | async-start | bytes 1179648 | tf_op jit(solution)/shard_map/all_to_all | solution.py:208
  27.4 171.1 %reduce-scatter.2.cloned.1.call-start = ((), (), s32[]{:S(2)}) async-start(), calls=%async_computation.5 | async-start | bytes 6815744 | tf_op jit(solution)/shard_map/reduce_scatter | solution.py:271
  52.3 0.8 copy-start
  85.0 13.5 %copy-start.3 = (s32[1,24]{1,0:T(1,128)S(1)}, s32[1,24]{1,0:T(1,128)}, u32[]{:S(2)}) copy-start(s32[1,24]{1,0:T(1,128)} %param.12) | copy-start | bytes 292
  92.1 9.6 %collective-permute-start = (bf16[12,2,32,1024]{3,2,1,0:T(8,128)(2,1)}, bf16[12,2,32,1024]{3,2,1,0:T(8,128)(2,1)S(1)}, u32[]{:S(2)}, u32[]{:S(2)}) collective-permute-start(bf16[12,2,32,1024]{3,2,1,0:T(8,128)(2,1)} %get-tuple-element.15), channel_id=1, source_target_pairs={{0,1},{1,0},{2,3},{3,2},{4,5},{5,4},{6,7},{7,6},{8,9},{9,8},{10,11... | collective-permute-start | bytes 4718600 | tf_op jit(solution)/shard_map/ppermute | solution.py:256
  101.7 1.2 copy-start.1
  112.9 1.0 copy-start.2
Sparse Core Ops, SparseCore 0:
  113.1 85.4 reduce-scatter.1

commit v2 on v1

--- a/solution.py
+++ b/solution.py
@@ -53,19 +53,53 @@
     return jnp.sum(jnp.where(same & before, 1.0, 0.0), axis=0, keepdims=True)
 
 
-def send_kernel(place_ref, slots_ref, inputs_ref, grads_ref, gate_ref, rows_ref, pick_ref):
-    own = place_ref[0] * GRP + place_ref[1]
+def send_kernel(
+    slots_hbm, inputs_hbm, grads_hbm, gate_hbm, rows_hbm, pick_ref,
+    slots_ref, inputs_ref, grads_ref, gate_ref, left_ref, right_ref, sems
+):
+    own = lax.axis_index("ep") * GRP + lax.axis_index("grp")
+    tile = pl.multiple_of((own // 8) * 8, 8)
+    loads = [
+        pltpu.make_async_copy(source, target, sems.at[k])
+        for k, (source, target) in enumerate(
+            (
+                (slots_hbm.at[pl.ds(tile, 8)], slots_ref),
+                (inputs_hbm, inputs_ref),
+                (gate_hbm, gate_ref),
+                (grads_hbm, grads_ref),
+            )
+        )
+    ]
+    for load in loads:
+        load.start()
+    loads[0].wait()
     slots = slots_ref[pl.ds(own % 8, 1), :]
     dest = split_slot(slots)[1].astype(f32)
     spot = dest * CAP + earlier_equal(dest)
     pick = (iota((ROWS_MID, TOK), 0).astype(f32) == spot).astype(bf16)
     pick_ref[...] = pick
+    loads[1].wait()
+    left_ref[...] = jnp.dot(pick, inputs_ref[...], preferred_element_type=f32).astype(bf16)
+    left = pltpu.make_async_copy(left_ref, rows_hbm.at[:, pl.ds(0, D)], sems.at[4])
+    left.start()
+    loads[2].wait()
+    loads[3].wait()
     scaled = (to_column(gate_ref[...]) * grads_ref[...].astype(f32)).astype(bf16)
-    rows_ref[:, :D] = jnp.dot(pick, inputs_ref[...], preferred_element_type=f32).astype(bf16)
-    rows_ref[:, D:] = jnp.dot(pick, scaled, preferred_element_type=f32).astype(bf16)
-
-
-def route_kernel(place_ref, block_ref, slots_ref, capacity_ref, forward_ref, kept_ref, wide_ref):
+    right_ref[...] = jnp.dot(pick, scaled, preferred_element_type=f32).astype(bf16)
+    right = pltpu.make_async_copy(right_ref, rows_hbm.at[:, pl.ds(D, D)], sems.at[5])
+    right.start()
+    left.wait()
+    right.wait()
+
+
+def route_kernel(
+    place_ref, block_ref, slots_ref, capacity_ref, forward_ref, kept_ref, blank_hbm,
+    wide_ref, zero_ref, sem
+):
+    zero_ref[...] = jnp.zeros_like(zero_ref)
+    fills = [pltpu.make_async_copy(zero_ref, blank_hbm.at[z], sem.at[z]) for z in range(Z)]
+    for fill in fills:
+        fill.start()
     grp_index = place_ref[1]
     col, row = split_slot(block_ref[...])
     hit = jnp.where(row == grp_index, 1.0, 0.0)
@@ -95,14 +129,12 @@
     counts = jnp.dot(arrived, jnp.ones((TOK, TOK), bf16), preferred_element_type=f32)
     lower = (iota((EP, EP), 1) < iota((EP, EP), 0)).astype(bf16)
     starts = jnp.dot(lower, counts.astype(bf16), preferred_element_type=f32)
-    capacity = capacity_ref[0].astype(f32)
+    capacity = capacity_ref[0, 0].astype(f32)
     for e in range(EP):
         kept = (lane < counts[e : e + 1, :]) & (starts[e : e + 1, :] + lane < capacity)
         kept_ref[e * CAP : (e + 1) * CAP, :] = jnp.where(kept, 1.0, 0.0)
-
-
-def forward_kernel(forward_ref, rows_ref, out_ref):
-    out_ref[...] = jnp.dot(forward_ref[...], rows_ref[...], preferred_element_type=f32).astype(bf16)
+    for fill in fills:
+        fill.wait()
 
 
 def back_kernel(pick_ref, rows_ref, out_ref):
@@ -123,40 +155,63 @@
 
 
 def slot_kernel(
-    place_ref, rows_ref, kept_ref, first_ref, second_ref, back_ref, mine_ref, other_ref, grad_ref
+    experts_ref, rows_hbm, kept_hbm, first_hbm, second_hbm, blank_hbm,
+    back_ref, merged_hbm, mine_hbm, other_hbm,
+    rows_ref, kept_ref, first_ref, second_ref, grad_refs, sems
 ):
-    core = place_ref[1] % 2
+    grp_index = lax.axis_index("grp")
+    core = grp_index % 2
+    expert = experts_ref[0, grp_index] - lax.axis_index("ep") * EXP_COL
+    loads = [
+        pltpu.make_async_copy(source, target, sems.at[k])
+        for k, (source, target) in enumerate(
+            (
+                (rows_hbm, rows_ref),
+                (kept_hbm, kept_ref),
+                (first_hbm, first_ref),
+                (second_hbm, second_ref),
+            )
+        )
+    ]
+    for load in loads:
+        load.start()
+    loads[0].wait()
+    loads[1].wait()
     kept = kept_ref[:, 0:1] > 0.0
     inputs = jnp.where(kept, rows_ref[:, :D].astype(f32), 0.0).astype(bf16)
     grads = jnp.where(kept, rows_ref[:, D:].astype(f32), 0.0).astype(bf16)
+
+    def store(k, left, right):
+        grad = lax.dot_general(left, right, (((0,), (0,)), ((), ())), preferred_element_type=f32)
+        grad_refs[k] = grad.astype(bf16).reshape(Z, 2, FEAT, FF)
+        copies = (
+            pltpu.make_async_copy(
+                grad_refs.at[k, :, 1 - core], other_hbm.at[:, k], sems.at[4 + 3 * k]
+            ),
+            pltpu.make_async_copy(
+                grad_refs.at[k, :, core], merged_hbm.at[:, k, expert], sems.at[5 + 3 * k]
+            ),
+            pltpu.make_async_copy(
+                grad_refs.at[k, :, core], mine_hbm.at[:, k], sems.at[6 + 3 * k]
+            ),
+        )
+        for copy in copies:
+            copy.start()
+        return copies
+
+    loads[2].wait()
     preact = jnp.dot(inputs, first_ref[...], preferred_element_type=f32)
+    gelu_value, gelu_slope = gelu_pair(preact)
+    stores = store(1, grads, gelu_value.astype(bf16))
+    loads[3].wait()
     hidden_grad = jnp.dot(grads, second_ref[...], preferred_element_type=f32)
-    gelu_value, gelu_slope = gelu_pair(preact)
-    activated = gelu_value.astype(bf16)
     preact_grad = (hidden_grad * gelu_slope).astype(bf16)
-    for k, (left, right) in enumerate(((inputs, preact_grad), (grads, activated))):
-        grad_ref[...] = lax.dot_general(
-            left, right, (((0,), (0,)), ((), ())), preferred_element_type=f32
-        ).astype(bf16)
-        for z in range(Z):
-            start = z * 2 * FEAT
-            mine = pl.multiple_of(start + core * FEAT, FEAT)
-            other = pl.multiple_of(start + (1 - core) * FEAT, FEAT)
-            mine_ref[z, k] = grad_ref[pl.ds(mine, FEAT), :]
-            other_ref[z, k] = grad_ref[pl.ds(other, FEAT), :]
+    stores += store(0, inputs, preact_grad)
     back_ref[...] = lax.dot_general(
         preact_grad, first_ref[...], (((1,), (1,)), ((), ())), preferred_element_type=f32
     ).astype(bf16)
-
-
-def merge_kernel(owner_ref, mine_ref, partner_ref, out_ref):
-    for k in range(2):
-        mine = mine_ref[0, k].astype(f32)
-        partner = partner_ref[0, k].astype(f32)
-        for e in range(EXP_COL):
-            first = jnp.where(owner_ref[0] == e, mine, 0.0)
-            second = jnp.where(owner_ref[1] == e, partner, 0.0)
-            out_ref[0, k, e] = (first + second).astype(bf16)
+    for copy in stores:
+        copy.wait()
 
 
 def shape(dims, dtype=bf16):
@@ -169,6 +224,10 @@
 
 def scalars():
     return pl.BlockSpec(memory_space=pltpu.SMEM)
+
+
+def anywhere():
+    return pl.BlockSpec(memory_space=pl.ANY)
 
 
 def per_device(
@@ -188,28 +247,25 @@
 
     rows_out, pick = pl.pallas_call(
         send_kernel,
-        grid_spec=pltpu.PrefetchScalarGridSpec(
-            num_scalar_prefetch=1,
-            grid=(1,),
-            in_specs=[
-                pl.BlockSpec((8, TOK), lambda i, p: ((p[0] * GRP + p[1]) // 8, 0)),
-                pl.BlockSpec((TOK, D), lambda i, p: (0, 0)),
-                pl.BlockSpec((TOK, D), lambda i, p: (0, 0)),
-                pl.BlockSpec((1, TOK), lambda i, p: (0, 0)),
-            ],
-            out_specs=[
-                pl.BlockSpec((ROWS_MID, 2 * D), lambda i, p: (0, 0)),
-                pl.BlockSpec((ROWS_MID, TOK), lambda i, p: (0, 0)),
-            ],
-        ),
+        in_specs=[anywhere()] * 4,
+        out_specs=[anywhere(), whole()],
         out_shape=[shape((ROWS_MID, 2 * D)), shape((ROWS_MID, TOK))],
+        scratch_shapes=[
+            pltpu.VMEM((8, TOK), i32),
+            pltpu.VMEM((TOK, D), bf16),
+            pltpu.VMEM((TOK, D), bf16),
+            pltpu.VMEM((1, TOK), f32),
+            pltpu.VMEM((ROWS_MID, D), bf16),
+            pltpu.VMEM((ROWS_MID, D), bf16),
+            pltpu.SemaphoreType.DMA((6,)),
+        ],
         name="send",
-    )(place, slots, token_inputs, output_grads, gate_probs.reshape(1, TOK))
+    )(slots, token_inputs, output_grads, gate_probs.reshape(1, TOK))
     rows_mid = lax.all_to_all(
         rows_out.reshape(GRP, CAP, 2 * D), "grp", split_axis=0, concat_axis=0, tiled=True
     ).reshape(ROWS_MID, 2 * D)
 
-    forward, kept = pl.pallas_call(
+    forward, kept, blank = pl.pallas_call(
         route_kernel,
         grid_spec=pltpu.PrefetchScalarGridSpec(
             num_scalar_prefetch=1,
@@ -222,52 +278,65 @@
             out_specs=[
                 pl.BlockSpec((ROWS_SLOT, ROWS_MID), lambda i, p: (0, 0)),
                 pl.BlockSpec((ROWS_SLOT, TOK), lambda i, p: (0, 0)),
+                anywhere(),
             ],
-            scratch_shapes=[pltpu.VMEM((ROWS_MID, TOK), f32)],
+            scratch_shapes=[
+                pltpu.VMEM((ROWS_MID, TOK), f32),
+                pltpu.VMEM((2, EXP_COL, FEAT, FF), bf16),
+                pltpu.SemaphoreType.DMA((Z,)),
+            ],
         ),
-        out_shape=[shape((ROWS_SLOT, ROWS_MID)), shape((ROWS_SLOT, TOK), f32)],
+        out_shape=[
+            shape((ROWS_SLOT, ROWS_MID)),
+            shape((ROWS_SLOT, TOK), f32),
+            shape((Z, 2, EXP_COL, FEAT, FF)),
+        ],
         name="route",
-    )(place, slots, slots, slot_capacity.reshape(1))
-
-    rows_fwd = pl.pallas_call(
-        forward_kernel,
-        in_specs=[whole(), whole()],
-        out_specs=whole(),
-        out_shape=shape((ROWS_SLOT, 2 * D)),
-        name="forward",
-    )(forward, rows_mid)
+    )(place, slots, slots, slot_capacity)
+
+    rows_fwd = jnp.dot(forward, rows_mid, preferred_element_type=f32).astype(bf16)
     rows_slot = lax.all_to_all(
         rows_fwd.reshape(EP, CAP, 2 * D), "ep", split_axis=0, concat_axis=0, tiled=True
     ).reshape(ROWS_SLOT, 2 * D)
 
-    back_rows, mine, other = pl.pallas_call(
+    back_rows, merged, mine, other = pl.pallas_call(
         slot_kernel,
-        in_specs=[scalars()] + [whole()] * 4,
-        out_specs=[whole()] * 3,
+        in_specs=[scalars()] + [anywhere()] * 5,
+        out_specs=[whole(), anywhere(), anywhere(), anywhere()],
         out_shape=[
             shape((ROWS_SLOT, D)),
+            shape((Z, 2, EXP_COL, FEAT, FF)),
             shape((Z, 2, FEAT, FF)),
             shape((Z, 2, FEAT, FF)),
         ],
-        scratch_shapes=[pltpu.VMEM((D, FF), bf16)],
+        scratch_shapes=[
+            pltpu.VMEM((ROWS_SLOT, 2 * D), bf16),
+            pltpu.VMEM((ROWS_SLOT, TOK), f32),
+            pltpu.VMEM((D, FF), bf16),
+            pltpu.VMEM((D, FF), bf16),
+            pltpu.VMEM((2, Z, 2, FEAT, FF), bf16),
+            pltpu.SemaphoreType.DMA((10,)),
+        ],
+        input_output_aliases={5: 1},
         name="slot",
-    )(place, rows_slot, kept, weight_in.reshape(D, FF), weight_out.reshape(D, FF))
+    )(
+        slot_experts,
+        rows_slot,
+        kept,
+        weight_in.reshape(D, FF),
+        weight_out.reshape(D, FF),
+        blank,
+    )
 
     partner = lax.ppermute(other, "grp", [(g, g ^ 1) for g in range(GRP)])
-    experts = slot_experts.reshape(GRP) - ep_index * EXP_COL
-    owners = lax.dynamic_slice_in_dim(experts, (grp_index // 2) * 2, 2)
-    owners = jnp.where(grp_index % 2 == 0, owners, owners[::-1])
-    merged = pl.pallas_call(
-        merge_kernel,
-        grid_spec=pltpu.PrefetchScalarGridSpec(
-            num_scalar_prefetch=1,
-            grid=(Z,),
-            in_specs=[pl.BlockSpec((1, 2, FEAT, FF), lambda i, p: (i, 0, 0, 0))] * 2,
-            out_specs=pl.BlockSpec((1, 2, EXP_COL, FEAT, FF), lambda i, p: (i, 0, 0, 0, 0)),
-        ),
-        out_shape=shape((Z, 2, EXP_COL, FEAT, FF)),
-        name="merge",
-    )(owners, mine, partner)
+    experts = slot_experts.reshape(GRP)
+    mine_expert = lax.dynamic_index_in_dim(experts, grp_index, keepdims=False)
+    partner_expert = lax.dynamic_index_in_dim(
+        experts, grp_index + 1 - 2 * (grp_index % 2), keepdims=False
+    )
+    local = partner_expert - ep_index * EXP_COL
+    total = partner.astype(f32) + jnp.where(mine_expert == partner_expert, mine.astype(f32), 0.0)
+    merged = lax.dynamic_update_index_in_dim(merged, total.astype(bf16), local, axis=2)
     expert_grads = lax.psum_scatter(
         merged.reshape(Z * 2 * EXP_COL * FEAT, FF),
         "grp",

time: 206 us -> 195 us (0.947)
  Pallas kernels: 29.1 us -> 19.6 us
  waiting for transfers between devices: 59 us -> 53.8 us
  other arithmetic: 1.26 us -> 3.89 us
    pallas_call x4 -> x2, Pallas kernels: 22.4 us -> 10.1 us  [the longest x1 7.14 us: per_device(): pl.pallas_call(slot_kernel, in_specs=[scalars()] + [anywhere()] * 5, out_...]
    all_to_all x1, waiting for transfers between devices: 21.4 us -> 18 us  [per_device(): lax.all_to_all(rows_out.reshape(GRP, CAP, 2 * D), 'grp', split_axis=0, co...]
    dynamic_update_slice x0 -> x1, other arithmetic: none -> 3.25 us  [per_device(): lax.dynamic_update_index_in_dim(merged, total.astype(bf16), local, axis=2)]
    pallas_call x1, Pallas kernels: 2.76 us -> 5.5 us  [per_device(): pl.pallas_call(route_kernel, grid_spec=pltpu.PrefetchScalarGridSpec(num_s...]
    unnamed x8 -> x4, local copies, waits for them, and re-layouts: 3.06 us -> 0.97 us
  transfers between devices with their start and end apart: 3 -> 3, of which waited for: 3 -> 3; matrix products, arithmetic and copies ran while one was open for 0% -> 1% of each run, Pallas kernels for 3% -> 5%
where the time goes in v2:
time: 195 us
  blocking collectives  74.8 us (38%)
  waiting for transfers between devices  53.8 us (28%)
  starting transfers between devices  23.1 us (12%)
  Pallas kernels  19.6 us (10%)
  between operations  16.7 us (9%)
  other arithmetic  3.89 us (2%)
    reduce_scatter x1, waiting for transfers between devices, per_device(): lax.psum_scatter(merged.reshape(Z * 2 * EXP_COL * FEAT, FF), 'grp', scatt...  35.1 us
    all_to_all x1, blocking collectives, per_device(): lax.all_to_all(rows_fwd.reshape(EP, CAP, 2 * D), 'ep', split_axis=0, conc...  29.3 us
    all_to_all x1, blocking collectives, per_device(): lax.all_to_all(source_back.reshape(GRP, CAP, D), 'grp', split_axis=0, con...  27.2 us
    all_to_all x1, blocking collectives, per_device(): lax.all_to_all(back_rows.reshape(EP, CAP, D), 'ep', split_axis=0, concat_...  18.3 us
    all_to_all x1, waiting for transfers between devices, per_device(): lax.all_to_all(rows_out.reshape(GRP, CAP, 2 * D), 'grp', split_axis=0, co...  18 us
    all_to_all x1, starting transfers between devices, per_device(): lax.all_to_all(rows_out.reshape(GRP, CAP, 2 * D), 'grp', split_axis=0, co...  16.7 us
    pallas_call x1, Pallas kernels, per_device(): pl.pallas_call(slot_kernel, in_specs=[scalars()] + [anywhere()] * 5, out_...  7.14 us
    ppermute x1, starting transfers between devices, per_device(): partner = lax.ppermute(other, 'grp', [(g, g ^ 1) for g in range(GRP)])  6.35 us
  transfers between devices with their start and end apart: 3, of which 3 were waited for; matrix products, arithmetic and copies ran while one was open for 1% of the time, Pallas kernels for 5%

profile of v2, /device:TPU:1, one launch (start us, length us, event | category | flops | bytes accessed | tf_op | source)
XLA Modules:
  0.0 194.7 jit_solution(12901898906571772322)
XLA Ops:
  7.2 3.0 %send.1 = (bf16[192,1536]{1,0:T(8,128)(2,1)}, bf16[192,128]{1,0:T(8,128)(2,1)}) custom-call(s32[768,128]{1,0:T(8,128)} %bitcast.29, bf16[128,768]{1,0:T(8,128)(2,1)} %inputs_hbm.1, bf16[128,768]{1,0:T(8,128)(2,1)} %grads_hbm.1, f32[1,128]{1,0:T(1,128)} %bitcast.40), custom_call_target="tpu_custom_call" | custom-call | tf_op jit(solution)/shard_map/send/pallas_call | solution.py:248
  10.1 16.7 %all-to-all-start = ((bf16[24,8,1536]{2,1,0:T(8,128)(2,1)}), bf16[24,8,1536]{2,1,0:T(8,128)(2,1)S(1)}, u32[]{:S(2)}, u32[]{:S(2)}) async-start(bf16[24,8,1536]{2,1,0:T(8,128)(2,1)} %bitcast.38), calls=%async_computation | async-start | bytes 1179648 | tf_op jit(solution)/shard_map/all_to_all | solution.py:264
  26.8 0.0 reduce-scatter.2.cloned.1.call-start
  27.5 0.6 pad_add_fusion.place_ref
  28.2 5.5 %route.1 = (bf16[256,192]{1,0:T(8,128)(2,1)}, f32[256,128]{1,0:T(8,128)}, bf16[12,2,4,32,1024]{4,3,2,1,0:T(8,128)(2,1)}) custom-call(s32[2]{0:T(128)} %pad_add_fusion.place_ref, s32[768,128]{1,0:T(8,128)} %bitcast.30, s32[768,128]{1,0:T(8,128)} %bitcast.31, s32[1,1]{1,0:T(1,128)S(6)} %copy.14.capacity_ref), custom_call_target="tpu_custom_call" | custom-call | tf_op jit(solution)/shard_map/route/pallas_call | solution.py:268
  33.7 18.0 %all-to-all-done = bf16[24,8,1536]{2,1,0:T(8,128)(2,1)S(1)} async-done(((bf16[24,8,1536]{2,1,0:T(8,128)(2,1)}), bf16[24,8,1536]{2,1,0:T(8,128)(2,1)S(1)}, u32[]{:S(2)}, u32[]{:S(2)}) %all-to-all-start) | async-done | bytes 589856 | tf_op jit(solution)/shard_map/all_to_all | solution.py:264
  51.6 1.3 fusion
  52.9 29.3 %all_to_all.20 = bf16[32,8,1536]{2,1,0:T(8,128)(2,1)} all-to-all(bf16[32,8,1536]{2,1,0:T(8,128)(2,1)S(1)} %fusion), channel_id=1, replica_groups=mesh['ep'=32,'grp'=24] {'ep'}, dimensions={0} | all-to-all | bytes 1572864 | tf_op jit(solution)/shard_map/all_to_all | solution.py:298
  82.2 0.0 copy-start.1
  82.2 7.1 %slot.1 = (bf16[256,768]{1,0:T(8,128)(2,1)}, bf16[12,2,4,32,1024]{4,3,2,1,0:T(8,128)(2,1)}, bf16[12,2,32,1024]{3,2,1,0:T(8,128)(2,1)}, bf16[12,2,32,1024]{3,2,1,0:T(8,128)(2,1)}) custom-call(s32[1,24]{1,0:T(1,128)} %experts_ref.1, bf16[256,1536]{1,0:T(8,128)(2,1)} %bitcast.32, ...), custom_call_target="tpu_custom_call", output_to_operand_aliasing={{1}: (5, {})} | custom-call | tf_op jit(solution)/shard_map/slot/pallas_call | solution.py:302
  89.4 6.4 %collective-permute-start = (bf16[12,2,32,1024]{3,2,1,0:T(8,128)(2,1)}, bf16[12,2,32,1024]{3,2,1,0:T(8,128)(2,1)S(1)}, u32[]{:S(2)}, u32[]{:S(2)}) collective-permute-start(bf16[12,2,32,1024]{3,2,1,0:T(8,128)(2,1)} %get-tuple-element.18), channel_id=1, source_target_pairs={{0,1},{1,0},{2,3},{3,2},{4,5},{5,4},{6,7},{7,6},{8,9},{9,8},{10,11... | collective-permute-start | bytes 4718600 | tf_op jit(solution)/shard_map/ppermute | solution.py:331
  95.7 0.0 copy-done.1
  95.8 0.6 constant_dynamic-slice_fusion.1
  98.3 0.7 collective-permute-done
  98.9 3.2 %fusion.2 = bf16[12,2,4,32,1024]{4,3,2,1,0:T(8,128)(2,1)} fusion(bf16[12,2,4,32,1024]{4,3,2,1,0:T(8,128)(2,1)} %get-tuple-element.17, s32[]{:T(128)S(6)} %select_n.31, bf16[12,2,32,1024]{3,2,1,0:T(8,128)(2,1)} %get-tuple-element.19, bf16[12,2,32,1024]{3,2,1,0:T(8,128)(2,1)S(1)} %collective-permute-done, pred[]{:T(512)S(6)} %eq.5), kind=kLoop, calls=%fused_computation.4 | loop fusion | flops 3932160 | bytes 4718597 | tf_op jit(solution)/shard_map/jit(dynamic_update_index_in_dim)/dynamic_update_slice | solution.py:339
  102.2 0.0 copy-start
  102.2 0.0 reduce-scatter.2.cloned.1.call-update
  102.2 1.0 copy-done
  103.2 18.3 %all_to_all.21 = bf16[32,8,768]{2,1,0:T(8,128)(2,1)} all-to-all(bf16[32,8,768]{2,1,0:T(8,128)(2,1)S(1)} %bitcast.39), channel_id=1, replica_groups=mesh['ep'=32,'grp'=24] {'ep'}, dimensions={0} | all-to-all | bytes 786432 | tf_op jit(solution)/shard_map/all_to_all | solution.py:348
  121.5 2.1 %back_mid.1 = bf16[192,768]{1,0:T(8,128)(2,1)} custom-call(bf16[256,192]{1,0:T(8,128)(2,1)} %get-tuple-element.12.pick_ref, bf16[256,768]{1,0:T(8,128)(2,1)} %bitcast.33), custom_call_target="tpu_custom_call" | custom-call | tf_op jit(solution)/shard_map/back_mid/pallas_call | solution.py:351
  123.6 27.2 %all_to_all.22 = bf16[24,8,768]{2,1,0:T(8,128)(2,1)} all-to-all(bf16[24,8,768]{2,1,0:T(8,128)(2,1)} %bitcast.36), channel_id=1, replica_groups=mesh['ep'=32,'grp'=24] {'grp'}, dimensions={0} | all-to-all | bytes 589824 | tf_op jit(solution)/shard_map/all_to_all | solution.py:358
  150.8 1.9 back_own.1
  152.7 35.1 %reduce-scatter.2.cloned.1.call-done = bf16[256,1024]{1,0:T(8,128)(2,1)} async-done(((bf16[3072,1024]{1,0:T(8,128)(2,1)}), bf16[256,1024]{1,0:T(8,128)(2,1)}) %reduce-scatter.2.cloned.1.call-update) | async-done | bytes 524304 | tf_op jit(solution)/shard_map/reduce_scatter | solution.py:340
Async XLA Ops:
  10.1 41.5 %all-to-all-start = ((bf16[24,8,1536]{2,1,0:T(8,128)(2,1)}), bf16[24,8,1536]{2,1,0:T(8,128)(2,1)S(1)}, u32[]{:S(2)}, u32[]{:S(2)}) async-start(bf16[24,8,1536]{2,1,0:T(8,128)(2,1)} %bitcast.38), calls=%async_computation | async-start | bytes 1179648 | tf_op jit(solution)/shard_map/all_to_all | solution.py:264
  26.8 161.0 %reduce-scatter.2.cloned.1.call-start = ((), (), s32[]{:S(2)}) async-start(), calls=%async_computation.5 | async-start | bytes 6815744 | tf_op jit(solution)/shard_map/reduce_scatter | solution.py:340
  82.2 13.5 %copy-start.1 = (s32[1,24]{1,0:T(1,128)S(1)}, s32[1,24]{1,0:T(1,128)}, u32[]{:S(2)}) copy-start(s32[1,24]{1,0:T(1,128)} %experts_ref.1) | copy-start | bytes 292
  89.4 9.6 %collective-permute-start = (bf16[12,2,32,1024]{3,2,1,0:T(8,128)(2,1)}, bf16[12,2,32,1024]{3,2,1,0:T(8,128)(2,1)S(1)}, u32[]{:S(2)}, u32[]{:S(2)}) collective-permute-start(bf16[12,2,32,1024]{3,2,1,0:T(8,128)(2,1)} %get-tuple-element.18), channel_id=1, source_target_pairs={{0,1},{1,0},{2,3},{3,2},{4,5},{5,4},{6,7},{7,6},{8,9},{9,8},{10,11... | collective-permute-start | bytes 4718600 | tf_op jit(solution)/shard_map/ppermute | solution.py:331
  102.2 1.0 copy-start
Sparse Core Ops, SparseCore 0:
  102.3 85.4 reduce-scatter.1

commit v3 on v2

--- a/solution.py
+++ b/solution.py
@@ -154,20 +154,27 @@
     return gelu_value, gelu_slope
 
 
-def slot_kernel(
-    experts_ref, rows_hbm, kept_hbm, first_hbm, second_hbm, blank_hbm,
-    back_ref, merged_hbm, mine_hbm, other_hbm,
-    rows_ref, kept_ref, first_ref, second_ref, grad_refs, sems
+def grad_kernel(
+    experts_ref, rows_hbm, slope_hbm, act_hbm, other_rows_hbm, first_hbm, second_hbm, blank_hbm,
+    merged_hbm,
+    rows_ref, slope_ref, act_ref, other_rows_ref, first_ref, second_ref, across_ref, grad_ref,
+    load_sems, store_sems
 ):
     grp_index = lax.axis_index("grp")
     core = grp_index % 2
-    expert = experts_ref[0, grp_index] - lax.axis_index("ep") * EXP_COL
+    base = lax.axis_index("ep") * EXP_COL
+    owners = (
+        experts_ref[0, grp_index] - base,
+        experts_ref[0, grp_index + 1 - 2 * core] - base,
+    )
     loads = [
-        pltpu.make_async_copy(source, target, sems.at[k])
+        pltpu.make_async_copy(source, target, load_sems.at[k])
         for k, (source, target) in enumerate(
             (
                 (rows_hbm, rows_ref),
-                (kept_hbm, kept_ref),
+                (slope_hbm, slope_ref),
+                (act_hbm, act_ref),
+                (other_rows_hbm, other_rows_ref),
                 (first_hbm, first_ref),
                 (second_hbm, second_ref),
             )
@@ -175,43 +182,44 @@
     ]
     for load in loads:
         load.start()
+
+    def store(n, k):
+        copy = pltpu.make_async_copy(
+            grad_ref.at[n, k], merged_hbm.at[:, k, owners[n]], store_sems.at[n, k]
+        )
+        copy.start()
+        return copy
+
+    def halves(n, source):
+        for k in range(2):
+            across_ref[n, k] = source[:, k * D : (k + 1) * D].T.reshape(Z, 2, FEAT, ROWS_SLOT)
+        return [across_ref[n, k, :, core].reshape(D // 2, ROWS_SLOT) for k in range(2)]
+
     loads[0].wait()
-    loads[1].wait()
-    kept = kept_ref[:, 0:1] > 0.0
-    inputs = jnp.where(kept, rows_ref[:, :D].astype(f32), 0.0).astype(bf16)
-    grads = jnp.where(kept, rows_ref[:, D:].astype(f32), 0.0).astype(bf16)
-
-    def store(k, left, right):
-        grad = lax.dot_general(left, right, (((0,), (0,)), ((), ())), preferred_element_type=f32)
-        grad_refs[k] = grad.astype(bf16).reshape(Z, 2, FEAT, FF)
-        copies = (
-            pltpu.make_async_copy(
-                grad_refs.at[k, :, 1 - core], other_hbm.at[:, k], sems.at[4 + 3 * k]
-            ),
-            pltpu.make_async_copy(
-                grad_refs.at[k, :, core], merged_hbm.at[:, k, expert], sems.at[5 + 3 * k]
-            ),
-            pltpu.make_async_copy(
-                grad_refs.at[k, :, core], mine_hbm.at[:, k], sems.at[6 + 3 * k]
-            ),
-        )
-        for copy in copies:
-            copy.start()
-        return copies
-
-    loads[2].wait()
-    preact = jnp.dot(inputs, first_ref[...], preferred_element_type=f32)
+    lefts = halves(0, rows_ref)
+    stores = []
+    for k, source in enumerate((slope_ref, act_ref)):
+        loads[1 + k].wait()
+        grad = jnp.dot(lefts[k], source[...], preferred_element_type=f32)
+        grad_ref[0, k] = grad.astype(bf16).reshape(Z, FEAT, FF)
+        stores.append(store(0, k))
+    loads[3].wait()
+    loads[4].wait()
+    preact = jnp.dot(other_rows_ref[:, :D], first_ref[...], preferred_element_type=f32)
+    loads[5].wait()
+    hidden_grad = jnp.dot(other_rows_ref[:, D:], second_ref[...], preferred_element_type=f32)
+    lefts = halves(1, other_rows_ref)
     gelu_value, gelu_slope = gelu_pair(preact)
-    stores = store(1, grads, gelu_value.astype(bf16))
-    loads[3].wait()
-    hidden_grad = jnp.dot(grads, second_ref[...], preferred_element_type=f32)
-    preact_grad = (hidden_grad * gelu_slope).astype(bf16)
-    stores += store(0, inputs, preact_grad)
-    back_ref[...] = lax.dot_general(
-        preact_grad, first_ref[...], (((1,), (1,)), ((), ())), preferred_element_type=f32
-    ).astype(bf16)
-    for copy in stores:
-        copy.wait()
+    rights = ((hidden_grad * gelu_slope).astype(bf16), gelu_value.astype(bf16))
+    same = owners[0] == owners[1]
+    for k in (1, 0):
+        grad = jnp.dot(lefts[k], rights[k], preferred_element_type=f32)
+        held = jnp.where(same, grad_ref[0, k].reshape(D // 2, FF).astype(f32), 0.0)
+        grad_ref[1, k] = (grad + held).astype(bf16).reshape(Z, FEAT, FF)
+        stores[k].wait()
+        stores.append(store(1, k))
+    stores[2].wait()
+    stores[3].wait()
 
 
 def shape(dims, dtype=bf16):
@@ -299,44 +307,50 @@
         rows_fwd.reshape(EP, CAP, 2 * D), "ep", split_axis=0, concat_axis=0, tiled=True
     ).reshape(ROWS_SLOT, 2 * D)
 
-    back_rows, merged, mine, other = pl.pallas_call(
-        slot_kernel,
-        in_specs=[scalars()] + [anywhere()] * 5,
-        out_specs=[whole(), anywhere(), anywhere(), anywhere()],
-        out_shape=[
-            shape((ROWS_SLOT, D)),
-            shape((Z, 2, EXP_COL, FEAT, FF)),
-            shape((Z, 2, FEAT, FF)),
-            shape((Z, 2, FEAT, FF)),
-        ],
+    first = weight_in.reshape(D, FF)
+    second = weight_out.reshape(D, FF)
+    early_first, early_second, _ = lax.optimization_barrier((first, second, forward))
+    swap = [(g, g ^ 1) for g in range(GRP)]
+    other_first = lax.ppermute(early_first, "grp", swap)
+    other_second = lax.ppermute(early_second, "grp", swap)
+    rows_kept = jnp.where(kept[:, 0:1] > 0.0, rows_slot, jnp.zeros_like(rows_slot))
+    other_rows = lax.ppermute(rows_kept, "grp", swap)
+    preact = jnp.dot(rows_kept[:, :D], first, preferred_element_type=f32)
+    gelu_value, gelu_slope = gelu_pair(preact)
+    hidden_grad = jnp.dot(rows_kept[:, D:], second, preferred_element_type=f32)
+    preact_grad = (hidden_grad * gelu_slope).astype(bf16)
+    merged = pl.pallas_call(
+        grad_kernel,
+        in_specs=[scalars()] + [anywhere()] * 7,
+        out_specs=anywhere(),
+        out_shape=shape((Z, 2, EXP_COL, FEAT, FF)),
         scratch_shapes=[
             pltpu.VMEM((ROWS_SLOT, 2 * D), bf16),
-            pltpu.VMEM((ROWS_SLOT, TOK), f32),
+            pltpu.VMEM((ROWS_SLOT, FF), bf16),
+            pltpu.VMEM((ROWS_SLOT, FF), bf16),
+            pltpu.VMEM((ROWS_SLOT, 2 * D), bf16),
             pltpu.VMEM((D, FF), bf16),
             pltpu.VMEM((D, FF), bf16),
-            pltpu.VMEM((2, Z, 2, FEAT, FF), bf16),
-            pltpu.SemaphoreType.DMA((10,)),
+            pltpu.VMEM((2, 2, Z, 2, FEAT, ROWS_SLOT), bf16),
+            pltpu.VMEM((2, 2, Z, FEAT, FF), bf16),
+            pltpu.SemaphoreType.DMA((6,)),
+            pltpu.SemaphoreType.DMA((2, 2)),
         ],
-        input_output_aliases={5: 1},
-        name="slot",
+        input_output_aliases={7: 0},
+        name="grad",
     )(
         slot_experts,
-        rows_slot,
-        kept,
-        weight_in.reshape(D, FF),
-        weight_out.reshape(D, FF),
+        rows_kept,
+        preact_grad,
+        gelu_value.astype(bf16),
+        other_rows,
+        other_first,
+        other_second,
         blank,
     )
-
-    partner = lax.ppermute(other, "grp", [(g, g ^ 1) for g in range(GRP)])
-    experts = slot_experts.reshape(GRP)
-    mine_expert = lax.dynamic_index_in_dim(experts, grp_index, keepdims=False)
-    partner_expert = lax.dynamic_index_in_dim(
-        experts, grp_index + 1 - 2 * (grp_index % 2), keepdims=False
-    )
-    local = partner_expert - ep_index * EXP_COL
-    total = partner.astype(f32) + jnp.where(mine_expert == partner_expert, mine.astype(f32), 0.0)
-    merged = lax.dynamic_update_index_in_dim(merged, total.astype(bf16), local, axis=2)
+    back_rows = lax.dot_general(
+        preact_grad, first, (((1,), (1,)), ((), ())), preferred_element_type=f32
+    ).astype(bf16)
     expert_grads = lax.psum_scatter(
         merged.reshape(Z * 2 * EXP_COL * FEAT, FF),
         "grp",

time: 195 us -> 194 us (level)
  blocking collectives: 74.8 us -> 45.6 us
  starting transfers between devices: 23.1 us -> 39.4 us
  waiting for transfers between devices: 53.8 us -> 64.9 us
  matrix products: 1.26 us -> 6.15 us
  other arithmetic: 3.89 us -> 0.89 us
    all_to_all x1 -> x0, blocking collectives: 29.3 us -> none  [per_device(): lax.all_to_all(rows_fwd.reshape(EP, CAP, 2 * D), 'ep', split_axis=0, conc...]
    all_to_all x0 -> x1, waiting for transfers between devices: none -> 13.2 us  [per_device(): lax.all_to_all(rows_fwd.reshape(EP, CAP, 2 * D), 'ep', split_axis=0, conc...]
    all_to_all x0 -> x1, starting transfers between devices: none -> 9.66 us  [per_device(): lax.all_to_all(rows_fwd.reshape(EP, CAP, 2 * D), 'ep', split_axis=0, conc...]
    ppermute x1 -> x3, starting transfers between devices: 6.35 us -> 13 us  [the longest x1 6.63 us: per_device(): other_rows = lax.ppermute(rows_kept, 'grp', swap)]
    dot_general x0 -> x3, matrix products: none -> 3.93 us  [the longest x1 1.75 us: per_device(): hidden_grad = jnp.dot(rows_kept[:, D:], second, preferred_element_type=f32)]
    dynamic_update_slice x1 -> x0, other arithmetic: 3.25 us -> none  [per_device(): lax.dynamic_update_index_in_dim(merged, total.astype(bf16), local, axis=2)]
    unnamed x4 -> x16, local copies, waits for them, and re-layouts: 0.97 us -> 3.03 us
  transfers between devices with their start and end apart: 3 -> 6, of which waited for: 3 -> 3; matrix products, arithmetic and copies ran while one was open for 1% -> 2% of each run, Pallas kernels for 5% -> 5%
where the time goes in v3:
time: 194 us; the launch traced here: 193 us
  waiting for transfers between devices  64.9 us (33%)
  blocking collectives  45.6 us (24%)
  starting transfers between devices  39.4 us (20%)
  Pallas kernels  18.4 us (9%)
  between operations  14.9 us (8%)
  matrix products  6.15 us (3%)
  local copies, waits for them, and re-layouts  3.03 us (2%)
    reduce_scatter x1, waiting for transfers between devices, per_device(): lax.psum_scatter(merged.reshape(Z * 2 * EXP_COL * FEAT, FF), 'grp', scatt...  33.7 us
    all_to_all x1, blocking collectives, per_device(): lax.all_to_all(source_back.reshape(GRP, CAP, D), 'grp', split_axis=0, con...  26.8 us
    all_to_all x1, blocking collectives, per_device(): lax.all_to_all(back_rows.reshape(EP, CAP, D), 'ep', split_axis=0, concat_...  18.8 us
    all_to_all x1, waiting for transfers between devices, per_device(): lax.all_to_all(rows_out.reshape(GRP, CAP, 2 * D), 'grp', split_axis=0, co...  18 us
    all_to_all x1, starting transfers between devices, per_device(): lax.all_to_all(rows_out.reshape(GRP, CAP, 2 * D), 'grp', split_axis=0, co...  16.7 us
    all_to_all x1, waiting for transfers between devices, per_device(): lax.all_to_all(rows_fwd.reshape(EP, CAP, 2 * D), 'ep', split_axis=0, conc...  13.2 us
    all_to_all x1, starting transfers between devices, per_device(): lax.all_to_all(rows_fwd.reshape(EP, CAP, 2 * D), 'ep', split_axis=0, conc...  9.66 us
    ppermute x1, starting transfers between devices, per_device(): other_rows = lax.ppermute(rows_kept, 'grp', swap)  6.63 us
  transfers between devices with their start and end apart: 6, of which 3 were waited for; matrix products, arithmetic and copies ran while one was open for 2% of the time, Pallas kernels for 5%

profile of v3, /device:TPU:1, one launch (start us, length us, event | category | flops | bytes accessed | tf_op | source)
XLA Modules:
  0.0 193.1 jit_solution(4149522919536821621)
XLA Ops:
  7.2 2.9 %send.1 = (bf16[192,1536]{1,0:T(8,128)(2,1)}, bf16[192,128]{1,0:T(8,128)(2,1)}) custom-call(s32[768,128]{1,0:T(8,128)} %bitcast.32, bf16[128,768]{1,0:T(8,128)(2,1)} %inputs_hbm.1, bf16[128,768]{1,0:T(8,128)(2,1)} %grads_hbm.1, f32[1,128]{1,0:T(1,128)} %bitcast.39), custom_call_target="tpu_custom_call" | custom-call | tf_op jit(solution)/shard_map/send/pallas_call | solution.py:256
  10.1 16.7 %all-to-all-start = ((bf16[24,8,1536]{2,1,0:T(8,128)(2,1)}), bf16[24,8,1536]{2,1,0:T(8,128)(2,1)S(1)}, u32[]{:S(2)}, u32[]{:S(2)}) async-start(bf16[24,8,1536]{2,1,0:T(8,128)(2,1)} %bitcast.38), calls=%async_computation | async-start | bytes 1179648 | tf_op jit(solution)/shard_map/all_to_all | solution.py:272
  27.5 0.7 pad_add_fusion.place_ref
  28.1 5.5 %route.1 = (bf16[256,192]{1,0:T(8,128)(2,1)}, f32[256,128]{1,0:T(8,128)}, bf16[12,2,4,32,1024]{4,3,2,1,0:T(8,128)(2,1)}) custom-call(s32[2]{0:T(128)} %pad_add_fusion.place_ref, s32[768,128]{1,0:T(8,128)} %bitcast.33, s32[768,128]{1,0:T(8,128)} %bitcast.34, s32[1,1]{1,0:T(1,128)S(6)} %copy.12.capacity_ref), custom_call_target="tpu_custom_call" | custom-call | tf_op jit(solution)/shard_map/route/pallas_call | solution.py:276
  33.6 18.0 %all-to-all-done = bf16[24,8,1536]{2,1,0:T(8,128)(2,1)S(1)} async-done(((bf16[24,8,1536]{2,1,0:T(8,128)(2,1)}), bf16[24,8,1536]{2,1,0:T(8,128)(2,1)S(1)}, u32[]{:S(2)}, u32[]{:S(2)}) %all-to-all-start) | async-done | bytes 589856 | tf_op jit(solution)/shard_map/all_to_all | solution.py:272
  51.6 2.2 %fusion = bf16[32,8,1536]{2,1,0:T(8,128)(2,1)} fusion(bf16[256,192]{1,0:T(8,128)(2,1)} %get-tuple-element.10.pick_ref, bf16[24,8,1536]{2,1,0:T(8,128)(2,1)S(1)} %all-to-all-done), kind=kOutput, calls=%fused_computation.1 | convolution fusion | flops 151388160 | bytes 1474560 | tf_op jit(solution)/shard_map/dot_general | solution.py:305
  53.8 9.7 %all-to-all-start.1 = ((bf16[32,8,1536]{2,1,0:T(8,128)(2,1)}), bf16[32,8,1536]{2,1,0:T(8,128)(2,1)S(1)}, u32[]{:S(2)}, u32[]{:S(2)}) async-start(bf16[32,8,1536]{2,1,0:T(8,128)(2,1)} %fusion), calls=%async_computation.1 | async-start | bytes 1572864 | tf_op jit(solution)/shard_map/all_to_all | solution.py:306
  63.6 4.4 %collective-permute-start.1 = (bf16[768,1024]{1,0:T(8,128)(2,1)}, bf16[768,1024]{1,0:T(8,128)(2,1)S(1)}, u32[]{:S(2)}, u32[]{:S(2)}) collective-permute-start(bf16[768,1024]{1,0:T(8,128)(2,1)} %bitcast.41), channel_id=1, source_target_pairs={{0,1},{1,0},{2,3},{3,2},{4,5},{5,4},{6,7},{7,6},{8,9},{9,8},{10,11... | collective-permute-start | bytes 4718600 | tf_op jit(solution)/shard_map/ppermute | solution.py:314
  68.0 1.9 collective-permute-start.2
  70.0 13.2 %all-to-all-done.1 = bf16[32,8,1536]{2,1,0:T(8,128)(2,1)S(1)} async-done(((bf16[32,8,1536]{2,1,0:T(8,128)(2,1)}), bf16[32,8,1536]{2,1,0:T(8,128)(2,1)S(1)}, u32[]{:S(2)}, u32[]{:S(2)}) %all-to-all-start.1) | async-done | bytes 786464 | tf_op jit(solution)/shard_map/all_to_all | solution.py:306
  83.4 6.6 %collective-permute-start = (bf16[256,1536]{1,0:T(8,128)(2,1)S(1)}, bf16[256,1536]{1,0:T(8,128)(2,1)S(1)}, u32[]{:S(2)}, u32[]{:S(2)}) collective-permute-start(bf16[256,1536]{1,0:T(8,128)(2,1)S(1)} %bitcast_select_fusion.rows_hbm), channel_id=1, source_target_pairs={{0,1},{1,0},{2,3},{3,2},{4,5},{5,4},{6,7},{7,6},{8,9},{9,8},{10,11... | collective-permute-start | bytes 2359304 | tf_op jit(solution)/shard_map/ppermute | solution.py:317
  90.0 1.6 multiply_convert_fusion
  91.6 1.7 fusion.1.slope_hbm
  93.4 1.2 copy-done.1
  94.6 0.3 copy-done.2
  94.9 6.0 %grad.1 = bf16[12,2,4,32,1024]{4,3,2,1,0:T(8,128)(2,1)} custom-call(s32[1,24]{1,0:T(1,128)} %experts_ref.1, bf16[256,1536]{1,0:T(8,128)(2,1)} %copy-done, bf16[256,1024]{1,0:T(8,128)(2,1)} %fusion.1.slope_hbm, bf16[256,1024]{1,0:T(8,128)(2,1)} %get-tuple-element.16.act_hbm, bf16[256,1536]{1,0:T(8,128)(2,1)} %copy-done.2, ...), custom_call_target="tpu_custom_call", output_to_operand_aliasing={{}: (7, {})} | custom-call | tf_op jit(solution)/shard_map/grad/pallas_call | solution.py:322
  100.9 1.0 copy-done.3
  101.9 0.5 copy-done.7
  102.5 0.6 fusion.2
  103.1 18.8 %all_to_all.20 = bf16[32,8,768]{2,1,0:T(8,128)(2,1)} all-to-all(bf16[32,8,768]{2,1,0:T(8,128)(2,1)S(1)} %fusion.2), channel_id=1, replica_groups=mesh['ep'=32,'grp'=24] {'ep'}, dimensions={0} | all-to-all | bytes 786432 | tf_op jit(solution)/shard_map/all_to_all | solution.py:362
  121.9 2.1 %back_mid.1 = bf16[192,768]{1,0:T(8,128)(2,1)} custom-call(bf16[256,192]{1,0:T(8,128)(2,1)} %get-tuple-element.10.pick_ref, bf16[256,768]{1,0:T(8,128)(2,1)} %bitcast.35), custom_call_target="tpu_custom_call" | custom-call | tf_op jit(solution)/shard_map/back_mid/pallas_call | solution.py:365
  124.0 26.8 %all_to_all.21 = bf16[24,8,768]{2,1,0:T(8,128)(2,1)} all-to-all(bf16[24,8,768]{2,1,0:T(8,128)(2,1)} %bitcast.36), channel_id=1, replica_groups=mesh['ep'=32,'grp'=24] {'grp'}, dimensions={0} | all-to-all | bytes 589824 | tf_op jit(solution)/shard_map/all_to_all | solution.py:372
  150.7 1.9 back_own.1
  152.6 33.7 %reduce-scatter.2.cloned.1.call-done = bf16[256,1024]{1,0:T(8,128)(2,1)} async-done(((bf16[3072,1024]{1,0:T(8,128)(2,1)}), bf16[256,1024]{1,0:T(8,128)(2,1)}) %reduce-scatter.2.cloned.1.call-update) | async-done | bytes 524304 | tf_op jit(solution)/shard_map/reduce_scatter | solution.py:354
  (19 shorter events, 0.3 us)
Async XLA Ops:
  10.1 41.5 %all-to-all-start = ((bf16[24,8,1536]{2,1,0:T(8,128)(2,1)}), bf16[24,8,1536]{2,1,0:T(8,128)(2,1)S(1)}, u32[]{:S(2)}, u32[]{:S(2)}) async-start(bf16[24,8,1536]{2,1,0:T(8,128)(2,1)} %bitcast.38), calls=%async_computation | async-start | bytes 1179648 | tf_op jit(solution)/shard_map/all_to_all | solution.py:272
  33.6 36.3 %copy-start.4 = (f32[256,128]{1,0:T(8,128)S(1)}, f32[256,128]{1,0:T(8,128)}, u32[]{:S(2)}) copy-start(f32[256,128]{1,0:T(8,128)} %get-tuple-element.11) | copy-start | bytes 393220
  53.8 29.4 %all-to-all-start.1 = ((bf16[32,8,1536]{2,1,0:T(8,128)(2,1)}), bf16[32,8,1536]{2,1,0:T(8,128)(2,1)S(1)}, u32[]{:S(2)}, u32[]{:S(2)}) async-start(bf16[32,8,1536]{2,1,0:T(8,128)(2,1)} %fusion), calls=%async_computation.1 | async-start | bytes 1572864 | tf_op jit(solution)/shard_map/all_to_all | solution.py:306
  63.5 122.8 %reduce-scatter.2.cloned.1.call-start = ((), (), s32[]{:S(2)}) async-start(), calls=%async_computation.5 | async-start | bytes 6815744 | tf_op jit(solution)/shard_map/reduce_scatter | solution.py:354
  63.6 29.8 %collective-permute-start.1 = (bf16[768,1024]{1,0:T(8,128)(2,1)}, bf16[768,1024]{1,0:T(8,128)(2,1)S(1)}, u32[]{:S(2)}, u32[]{:S(2)}) collective-permute-start(bf16[768,1024]{1,0:T(8,128)(2,1)} %bitcast.41), channel_id=1, source_target_pairs={{0,1},{1,0},{2,3},{3,2},{4,5},{5,4},{6,7},{7,6},{8,9},{9,8},{10,11... | collective-permute-start | bytes 4718600 | tf_op jit(solution)/shard_map/ppermute | solution.py:314
  68.0 25.4 %collective-permute-start.2 = (bf16[768,1024]{1,0:T(8,128)(2,1)}, bf16[768,1024]{1,0:T(8,128)(2,1)}, u32[]{:S(2)}, u32[]{:S(2)}) collective-permute-start(bf16[768,1024]{1,0:T(8,128)(2,1)} %bitcast.40), channel_id=1, source_target_pairs={{0,1},{1,0},{2,3},{3,2},{4,5},{5,4},{6,7},{7,6},{8,9},{9,8},{10,11... | collective-permute-start | bytes 4718600 | tf_op jit(solution)/shard_map/ppermute | solution.py:315
  83.2 6.8 %copy-start.6 = (bf16[1,1,768,1024]{3,2,1,0:T(8,128)(2,1)S(1)}, bf16[1,1,768,1024]{3,2,1,0:T(8,128)(2,1)}, u32[]{:S(2)}) copy-start(bf16[1,1,768,1024]{3,2,1,0:T(8,128)(2,1)} %param.14) | copy-start | bytes 4718596
  83.4 8.2 %copy-start = (bf16[256,1536]{1,0:T(8,128)(2,1)}, bf16[256,1536]{1,0:T(8,128)(2,1)S(1)}, u32[]{:S(2)}) copy-start(bf16[256,1536]{1,0:T(8,128)(2,1)S(1)} %bitcast_select_fusion.rows_hbm) | copy-start | bytes 2359300
  83.4 8.2 %copy-start.5 = (bf16[1,1,768,1024]{3,2,1,0:T(8,128)(2,1)S(1)}, bf16[1,1,768,1024]{3,2,1,0:T(8,128)(2,1)}, u32[]{:S(2)}) copy-start(bf16[1,1,768,1024]{3,2,1,0:T(8,128)(2,1)} %param.15) | copy-start | bytes 4718596
  83.4 10.0 %collective-permute-start = (bf16[256,1536]{1,0:T(8,128)(2,1)S(1)}, bf16[256,1536]{1,0:T(8,128)(2,1)S(1)}, u32[]{:S(2)}, u32[]{:S(2)}) collective-permute-start(bf16[256,1536]{1,0:T(8,128)(2,1)S(1)} %bitcast_select_fusion.rows_hbm), channel_id=1, source_target_pairs={{0,1},{1,0},{2,3},{3,2},{4,5},{5,4},{6,7},{7,6},{8,9},{9,8},{10,11... | collective-permute-start | bytes 2359304 | tf_op jit(solution)/shard_map/ppermute | solution.py:317
  93.4 1.2 copy-start.1
  93.4 1.5 copy-start.2
  100.9 1.0 copy-start.3
  100.9 1.6 copy-start.7
Sparse Core Ops, SparseCore 0:
  101.1 85.1 reduce-scatter.1

commit v4 on v3

--- a/solution.py
+++ b/solution.py
@@ -302,18 +302,21 @@
         name="route",
     )(place, slots, slots, slot_capacity)
 
-    rows_fwd = jnp.dot(forward, rows_mid, preferred_element_type=f32).astype(bf16)
-    rows_slot = lax.all_to_all(
-        rows_fwd.reshape(EP, CAP, 2 * D), "ep", split_axis=0, concat_axis=0, tiled=True
-    ).reshape(ROWS_SLOT, 2 * D)
-
     first = weight_in.reshape(D, FF)
     second = weight_out.reshape(D, FF)
     early_first, early_second, _ = lax.optimization_barrier((first, second, forward))
     swap = [(g, g ^ 1) for g in range(GRP)]
     other_first = lax.ppermute(early_first, "grp", swap)
     other_second = lax.ppermute(early_second, "grp", swap)
-    rows_kept = jnp.where(kept[:, 0:1] > 0.0, rows_slot, jnp.zeros_like(rows_slot))
+    rows_mid, other_first, other_second, kept_rows = lax.optimization_barrier(
+        (rows_mid, other_first, other_second, kept[:, 0] > 0.0)
+    )
+    rows_fwd = jnp.dot(forward, rows_mid, preferred_element_type=f32).astype(bf16)
+    rows_slot = lax.all_to_all(
+        rows_fwd.reshape(EP, CAP, 2 * D), "ep", split_axis=0, concat_axis=0, tiled=True
+    ).reshape(ROWS_SLOT, 2 * D)
+
+    rows_kept = jnp.where(kept_rows[:, None], rows_slot, jnp.zeros_like(rows_slot))
     other_rows = lax.ppermute(rows_kept, "grp", swap)
     preact = jnp.dot(rows_kept[:, :D], first, preferred_element_type=f32)
     gelu_value, gelu_slope = gelu_pair(preact)

time: 194 us -> 192 us (0.990)
  blocking collectives: 45.6 us -> 74.9 us
  waiting for transfers between devices: 64.9 us -> 46.4 us
  starting transfers between devices: 39.4 us -> 27.6 us
    all_to_all x0 -> x1, blocking collectives: none -> 29.3 us  [per_device(): lax.all_to_all(rows_fwd.reshape(EP, CAP, 2 * D), 'ep', split_axis=0, conc...]
    all_to_all x1 -> x0, waiting for transfers between devices: 13.2 us -> none  [per_device(): lax.all_to_all(rows_fwd.reshape(EP, CAP, 2 * D), 'ep', split_axis=0, conc...]
    all_to_all x1 -> x0, starting transfers between devices: 9.66 us -> none  [per_device(): lax.all_to_all(rows_fwd.reshape(EP, CAP, 2 * D), 'ep', split_axis=0, conc...]
    all_to_all x1, waiting for transfers between devices: 18 us -> 10.1 us  [per_device(): lax.all_to_all(rows_out.reshape(GRP, CAP, 2 * D), 'grp', split_axis=0, co...]
    ppermute x1, waiting for transfers between devices: 0.01 us -> 2.38 us  [per_device(): other_second = lax.ppermute(early_second, 'grp', swap)]
    ppermute x1, starting transfers between devices: 4.4 us -> 2.09 us  [per_device(): other_first = lax.ppermute(early_first, 'grp', swap)]
  transfers between devices with their start and end apart: 6 -> 5, of which waited for: 3 -> 4; matrix products, arithmetic and copies ran while one was open for 2% -> 3% of each run, Pallas kernels for 5% -> 5%
where the time goes in v4:
time: 192 us; the launch traced here: 191 us
  blocking collectives  74.9 us (39%)
  waiting for transfers between devices  46.4 us (24%)
  starting transfers between devices  27.6 us (14%)
  Pallas kernels  18.4 us (10%)
  between operations  14.8 us (8%)
  matrix products  5.18 us (3%)
  local copies, waits for them, and re-layouts  2.46 us (1%)
    reduce_scatter x1, waiting for transfers between devices, per_device(): lax.psum_scatter(merged.reshape(Z * 2 * EXP_COL * FEAT, FF), 'grp', scatt...  33.7 us
    all_to_all x1, blocking collectives, per_device(): lax.all_to_all(rows_fwd.reshape(EP, CAP, 2 * D), 'ep', split_axis=0, conc...  29.3 us
    all_to_all x1, blocking collectives, per_device(): lax.all_to_all(source_back.reshape(GRP, CAP, D), 'grp', split_axis=0, con...  26.8 us
    all_to_all x1, blocking collectives, per_device(): lax.all_to_all(back_rows.reshape(EP, CAP, D), 'ep', split_axis=0, concat_...  18.8 us
    all_to_all x1, starting transfers between devices, per_device(): lax.all_to_all(rows_out.reshape(GRP, CAP, 2 * D), 'grp', split_axis=0, co...  16.7 us
    all_to_all x1, waiting for transfers between devices, per_device(): lax.all_to_all(rows_out.reshape(GRP, CAP, 2 * D), 'grp', split_axis=0, co...  10.1 us
    ppermute x1, starting transfers between devices, per_device(): other_rows = lax.ppermute(rows_kept, 'grp', swap)  6.49 us
    pallas_call x1, Pallas kernels, per_device(): pl.pallas_call(grad_kernel, in_specs=[scalars()] + [anywhere()] * 7, out_...  6.04 us
  transfers between devices with their start and end apart: 5, of which 4 were waited for; matrix products, arithmetic and copies ran while one was open for 3% of the time, Pallas kernels for 5%

profile of v4, /device:TPU:1, one launch (start us, length us, event | category | flops | bytes accessed | tf_op | source)
XLA Modules:
  0.0 191.5 jit_solution(15556276757603015785)
XLA Ops:
  7.2 2.9 %send.1 = (bf16[192,1536]{1,0:T(8,128)(2,1)}, bf16[192,128]{1,0:T(8,128)(2,1)}) custom-call(s32[768,128]{1,0:T(8,128)} %bitcast.31, bf16[128,768]{1,0:T(8,128)(2,1)} %inputs_hbm.1, bf16[128,768]{1,0:T(8,128)(2,1)} %grads_hbm.1, f32[1,128]{1,0:T(1,128)} %bitcast.39), custom_call_target="tpu_custom_call" | custom-call | tf_op jit(solution)/shard_map/send/pallas_call | solution.py:256
  10.1 16.7 %all-to-all-start = ((bf16[24,8,1536]{2,1,0:T(8,128)(2,1)}), bf16[24,8,1536]{2,1,0:T(8,128)(2,1)S(1)}, u32[]{:S(2)}, u32[]{:S(2)}) async-start(bf16[24,8,1536]{2,1,0:T(8,128)(2,1)} %bitcast.38), calls=%async_computation | async-start | bytes 1179648 | tf_op jit(solution)/shard_map/all_to_all | solution.py:272
  27.5 0.6 pad_add_fusion.place_ref
  28.1 5.5 %route.1 = (bf16[256,192]{1,0:T(8,128)(2,1)}, f32[256,128]{1,0:T(8,128)}, bf16[12,2,4,32,1024]{4,3,2,1,0:T(8,128)(2,1)}) custom-call(s32[2]{0:T(128)} %pad_add_fusion.place_ref, s32[768,128]{1,0:T(8,128)} %bitcast.32, s32[768,128]{1,0:T(8,128)} %bitcast.33, s32[1,1]{1,0:T(1,128)S(6)} %copy.12.capacity_ref), custom_call_target="tpu_custom_call" | custom-call | tf_op jit(solution)/shard_map/route/pallas_call | solution.py:276
  33.6 2.1 %collective-permute-start = (bf16[768,1024]{1,0:T(8,128)(2,1)}, bf16[768,1024]{1,0:T(8,128)(2,1)S(1)}, u32[]{:S(2)}, u32[]{:S(2)}) collective-permute-start(bf16[768,1024]{1,0:T(8,128)(2,1)} %bitcast.41), channel_id=1, source_target_pairs={{0,1},{1,0},{2,3},{3,2},{4,5},{5,4},{6,7},{7,6},{8,9},{9,8},{10,11... | collective-permute-start | bytes 4718600 | tf_op jit(solution)/shard_map/ppermute | solution.py:309
  35.7 2.2 %collective-permute-start.1 = (bf16[768,1024]{1,0:T(8,128)(2,1)}, bf16[768,1024]{1,0:T(8,128)(2,1)}, u32[]{:S(2)}, u32[]{:S(2)}) collective-permute-start(bf16[768,1024]{1,0:T(8,128)(2,1)} %bitcast.40), channel_id=1, source_target_pairs={{0,1},{1,0},{2,3},{3,2},{4,5},{5,4},{6,7},{7,6},{8,9},{9,8},{10,11... | collective-permute-start | bytes 4718600 | tf_op jit(solution)/shard_map/ppermute | solution.py:310
  38.0 1.0 fusion.6
  39.1 2.4 %collective-permute-done.1.second_hbm = bf16[768,1024]{1,0:T(8,128)(2,1)} collective-permute-done((bf16[768,1024]{1,0:T(8,128)(2,1)}, bf16[768,1024]{1,0:T(8,128)(2,1)}, u32[]{:S(2)}, u32[]{:S(2)}) %collective-permute-start.1) | collective-permute-done | bytes 1572896 | tf_op jit(solution)/shard_map/ppermute | solution.py:310
  41.5 10.1 %all-to-all-done = bf16[24,8,1536]{2,1,0:T(8,128)(2,1)S(1)} async-done(((bf16[24,8,1536]{2,1,0:T(8,128)(2,1)}), bf16[24,8,1536]{2,1,0:T(8,128)(2,1)S(1)}, u32[]{:S(2)}, u32[]{:S(2)}) %all-to-all-start) | async-done | bytes 589856 | tf_op jit(solution)/shard_map/all_to_all | solution.py:272
  51.6 1.3 fusion
  52.9 29.3 %all_to_all.20 = bf16[32,8,1536]{2,1,0:T(8,128)(2,1)S(1)} all-to-all(bf16[32,8,1536]{2,1,0:T(8,128)(2,1)S(1)} %fusion), channel_id=1, replica_groups=mesh['ep'=32,'grp'=24] {'ep'}, dimensions={0} | all-to-all | bytes 1572864 | tf_op jit(solution)/shard_map/all_to_all | solution.py:315
  82.4 6.5 %collective-permute-start.2 = (bf16[256,1536]{1,0:T(8,128)(2,1)S(1)}, bf16[256,1536]{1,0:T(8,128)(2,1)S(1)}, u32[]{:S(2)}, u32[]{:S(2)}) collective-permute-start(bf16[256,1536]{1,0:T(8,128)(2,1)S(1)} %bitcast_select_fusion.rows_hbm), channel_id=1, source_target_pairs={{0,1},{1,0},{2,3},{3,2},{4,5},{5,4},{6,7},{7,6},{8,9},{9,8},{10,11... | collective-permute-start | bytes 2359304 | tf_op jit(solution)/shard_map/ppermute | solution.py:320
  88.9 1.6 multiply_convert_fusion
  90.5 1.7 fusion.1.slope_hbm
  92.2 0.9 copy-done.2
  93.1 6.0 %grad.1 = bf16[12,2,4,32,1024]{4,3,2,1,0:T(8,128)(2,1)} custom-call(s32[1,24]{1,0:T(1,128)} %experts_ref.1, bf16[256,1536]{1,0:T(8,128)(2,1)} %copy-done, bf16[256,1024]{1,0:T(8,128)(2,1)} %fusion.1.slope_hbm, bf16[256,1024]{1,0:T(8,128)(2,1)} %get-tuple-element.24.act_hbm, bf16[256,1536]{1,0:T(8,128)(2,1)} %copy-done.2, ...), custom_call_target="tpu_custom_call", output_to_operand_aliasing={{}: (7, {})} | custom-call | tf_op jit(solution)/shard_map/grad/pallas_call | solution.py:325
  99.2 1.0 copy-done.3
  100.2 0.5 copy-done.6
  100.8 0.6 fusion.2
  101.4 18.8 %all_to_all.21 = bf16[32,8,768]{2,1,0:T(8,128)(2,1)} all-to-all(bf16[32,8,768]{2,1,0:T(8,128)(2,1)S(1)} %fusion.2), channel_id=1, replica_groups=mesh['ep'=32,'grp'=24] {'ep'}, dimensions={0} | all-to-all | bytes 786432 | tf_op jit(solution)/shard_map/all_to_all | solution.py:365
  120.2 2.0 %back_mid.1 = bf16[192,768]{1,0:T(8,128)(2,1)} custom-call(bf16[256,192]{1,0:T(8,128)(2,1)} %get-tuple-element.14.pick_ref, bf16[256,768]{1,0:T(8,128)(2,1)} %bitcast.35), custom_call_target="tpu_custom_call" | custom-call | tf_op jit(solution)/shard_map/back_mid/pallas_call | solution.py:368
  122.2 26.8 %all_to_all.22 = bf16[24,8,768]{2,1,0:T(8,128)(2,1)} all-to-all(bf16[24,8,768]{2,1,0:T(8,128)(2,1)} %bitcast.36), channel_id=1, replica_groups=mesh['ep'=32,'grp'=24] {'grp'}, dimensions={0} | all-to-all | bytes 589824 | tf_op jit(solution)/shard_map/all_to_all | solution.py:375
  149.0 1.9 back_own.1
  150.9 33.7 %reduce-scatter.2.cloned.1.call-done = bf16[256,1024]{1,0:T(8,128)(2,1)} async-done(((bf16[3072,1024]{1,0:T(8,128)(2,1)}), bf16[256,1024]{1,0:T(8,128)(2,1)}) %reduce-scatter.2.cloned.1.call-update) | async-done | bytes 524304 | tf_op jit(solution)/shard_map/reduce_scatter | solution.py:357
  (16 shorter events, 0.4 us)
Async XLA Ops:
  10.1 41.5 %all-to-all-start = ((bf16[24,8,1536]{2,1,0:T(8,128)(2,1)}), bf16[24,8,1536]{2,1,0:T(8,128)(2,1)S(1)}, u32[]{:S(2)}, u32[]{:S(2)}) async-start(bf16[24,8,1536]{2,1,0:T(8,128)(2,1)} %bitcast.38), calls=%async_computation | async-start | bytes 1179648 | tf_op jit(solution)/shard_map/all_to_all | solution.py:272
  26.8 157.8 %reduce-scatter.2.cloned.1.call-start = ((), (), s32[]{:S(2)}) async-start(), calls=%async_computation.5 | async-start | bytes 6815744 | tf_op jit(solution)/shard_map/reduce_scatter | solution.py:357
  33.6 5.5 %collective-permute-start = (bf16[768,1024]{1,0:T(8,128)(2,1)}, bf16[768,1024]{1,0:T(8,128)(2,1)S(1)}, u32[]{:S(2)}, u32[]{:S(2)}) collective-permute-start(bf16[768,1024]{1,0:T(8,128)(2,1)} %bitcast.41), channel_id=1, source_target_pairs={{0,1},{1,0},{2,3},{3,2},{4,5},{5,4},{6,7},{7,6},{8,9},{9,8},{10,11... | collective-permute-start | bytes 4718600 | tf_op jit(solution)/shard_map/ppermute | solution.py:309
  35.7 5.8 %collective-permute-start.1 = (bf16[768,1024]{1,0:T(8,128)(2,1)}, bf16[768,1024]{1,0:T(8,128)(2,1)}, u32[]{:S(2)}, u32[]{:S(2)}) collective-permute-start(bf16[768,1024]{1,0:T(8,128)(2,1)} %bitcast.40), channel_id=1, source_target_pairs={{0,1},{1,0},{2,3},{3,2},{4,5},{5,4},{6,7},{7,6},{8,9},{9,8},{10,11... | collective-permute-start | bytes 4718600 | tf_op jit(solution)/shard_map/ppermute | solution.py:310
  39.1 43.2 %copy-start.1 = (bf16[768,1024]{1,0:T(8,128)(2,1)}, bf16[768,1024]{1,0:T(8,128)(2,1)S(1)}, u32[]{:S(2)}) copy-start(bf16[768,1024]{1,0:T(8,128)(2,1)S(1)} %collective-permute-done.first_hbm) | copy-start | bytes 4718596
  52.9 36.0 %copy-start.5 = (bf16[1,1,768,1024]{3,2,1,0:T(8,128)(2,1)S(1)}, bf16[1,1,768,1024]{3,2,1,0:T(8,128)(2,1)}, u32[]{:S(2)}) copy-start(bf16[1,1,768,1024]{3,2,1,0:T(8,128)(2,1)} %param.14) | copy-start | bytes 4718596
  82.4 8.1 %copy-start = (bf16[256,1536]{1,0:T(8,128)(2,1)}, bf16[256,1536]{1,0:T(8,128)(2,1)S(1)}, u32[]{:S(2)}) copy-start(bf16[256,1536]{1,0:T(8,128)(2,1)S(1)} %bitcast_select_fusion.rows_hbm) | copy-start | bytes 2359300
  82.4 8.1 %copy-start.4 = (bf16[1,1,768,1024]{3,2,1,0:T(8,128)(2,1)S(1)}, bf16[1,1,768,1024]{3,2,1,0:T(8,128)(2,1)}, u32[]{:S(2)}) copy-start(bf16[1,1,768,1024]{3,2,1,0:T(8,128)(2,1)} %param.15) | copy-start | bytes 4718596
  82.4 9.8 %collective-permute-start.2 = (bf16[256,1536]{1,0:T(8,128)(2,1)S(1)}, bf16[256,1536]{1,0:T(8,128)(2,1)S(1)}, u32[]{:S(2)}, u32[]{:S(2)}) collective-permute-start(bf16[256,1536]{1,0:T(8,128)(2,1)S(1)} %bitcast_select_fusion.rows_hbm), channel_id=1, source_target_pairs={{0,1},{1,0},{2,3},{3,2},{4,5},{5,4},{6,7},{7,6},{8,9},{9,8},{10,11... | collective-permute-start | bytes 2359304 | tf_op jit(solution)/shard_map/ppermute | solution.py:320
  92.2 0.9 copy-start.2
  99.2 1.0 copy-start.3
  99.2 1.6 copy-start.6
Sparse Core Ops, SparseCore 0:
  99.3 85.2 reduce-scatter.1

commit v5 on v4

--- a/solution.py
+++ b/solution.py
@@ -320,7 +320,8 @@
     other_rows = lax.ppermute(rows_kept, "grp", swap)
     preact = jnp.dot(rows_kept[:, :D], first, preferred_element_type=f32)
     gelu_value, gelu_slope = gelu_pair(preact)
-    hidden_grad = jnp.dot(rows_kept[:, D:], second, preferred_element_type=f32)
+    rows_later, other_rows = lax.optimization_barrier((rows_kept, other_rows))
+    hidden_grad = jnp.dot(rows_later[:, D:], second, preferred_element_type=f32)
     preact_grad = (hidden_grad * gelu_slope).astype(bf16)
     merged = pl.pallas_call(
         grad_kernel,

time: 192 us -> 192 us (level)
  transfers between devices with their start and end apart: 5 -> 5, of which waited for: 4 -> 5; matrix products, arithmetic and copies ran while one was open for 3% -> 2% of each run, Pallas kernels for 5% -> 5%
where the time goes in v5:
time: 192 us; the launch traced here: 191 us
  blocking collectives  74.9 us (39%)
  waiting for transfers between devices  47 us (24%)
  starting transfers between devices  27.6 us (14%)
  Pallas kernels  18.4 us (10%)
  between operations  14.8 us (8%)
  matrix products  5.18 us (3%)
    reduce_scatter x1, waiting for transfers between devices, per_device(): lax.psum_scatter(merged.reshape(Z * 2 * EXP_COL * FEAT, FF), 'grp', scatt...  34 us
    all_to_all x1, blocking collectives, per_device(): lax.all_to_all(rows_fwd.reshape(EP, CAP, 2 * D), 'ep', split_axis=0, conc...  29.3 us
    all_to_all x1, blocking collectives, per_device(): lax.all_to_all(source_back.reshape(GRP, CAP, D), 'grp', split_axis=0, con...  27.2 us
    all_to_all x1, blocking collectives, per_device(): lax.all_to_all(back_rows.reshape(EP, CAP, D), 'ep', split_axis=0, concat_...  18.3 us
    all_to_all x1, starting transfers between devices, per_device(): lax.all_to_all(rows_out.reshape(GRP, CAP, 2 * D), 'grp', split_axis=0, co...  16.7 us
    all_to_all x1, waiting for transfers between devices, per_device(): lax.all_to_all(rows_out.reshape(GRP, CAP, 2 * D), 'grp', split_axis=0, co...  10.1 us
    ppermute x1, starting transfers between devices, per_device(): other_rows = lax.ppermute(rows_kept, 'grp', swap)  6.49 us
    pallas_call x1, Pallas kernels, per_device(): pl.pallas_call(grad_kernel, in_specs=[scalars()] + [anywhere()] * 7, out_...  6.02 us
  transfers between devices with their start and end apart: 5, of which 5 were waited for; matrix products, arithmetic and copies ran while one was open for 2% of the time, Pallas kernels for 5%

profile of v5, /device:TPU:1, one launch (start us, length us, event | category | flops | bytes accessed | tf_op | source)
XLA Modules:
  0.0 191.1 jit_solution(17006653932536647521)
XLA Ops:
  7.2 2.9 %send.1 = (bf16[192,1536]{1,0:T(8,128)(2,1)}, bf16[192,128]{1,0:T(8,128)(2,1)}) custom-call(s32[768,128]{1,0:T(8,128)} %bitcast.31, bf16[128,768]{1,0:T(8,128)(2,1)} %inputs_hbm.1, bf16[128,768]{1,0:T(8,128)(2,1)} %grads_hbm.1, f32[1,128]{1,0:T(1,128)} %bitcast.39), custom_call_target="tpu_custom_call" | custom-call | tf_op jit(solution)/shard_map/send/pallas_call | solution.py:256
  10.1 16.7 %all-to-all-start = ((bf16[24,8,1536]{2,1,0:T(8,128)(2,1)}), bf16[24,8,1536]{2,1,0:T(8,128)(2,1)S(1)}, u32[]{:S(2)}, u32[]{:S(2)}) async-start(bf16[24,8,1536]{2,1,0:T(8,128)(2,1)} %bitcast.38), calls=%async_computation | async-start | bytes 1179648 | tf_op jit(solution)/shard_map/all_to_all | solution.py:272
  27.5 0.6 pad_add_fusion.place_ref
  28.1 5.5 %route.1 = (bf16[256,192]{1,0:T(8,128)(2,1)}, f32[256,128]{1,0:T(8,128)}, bf16[12,2,4,32,1024]{4,3,2,1,0:T(8,128)(2,1)}) custom-call(s32[2]{0:T(128)} %pad_add_fusion.place_ref, s32[768,128]{1,0:T(8,128)} %bitcast.32, s32[768,128]{1,0:T(8,128)} %bitcast.33, s32[1,1]{1,0:T(1,128)S(6)} %copy.12.capacity_ref), custom_call_target="tpu_custom_call" | custom-call | tf_op jit(solution)/shard_map/route/pallas_call | solution.py:276
  33.6 2.1 %collective-permute-start = (bf16[768,1024]{1,0:T(8,128)(2,1)}, bf16[768,1024]{1,0:T(8,128)(2,1)S(1)}, u32[]{:S(2)}, u32[]{:S(2)}) collective-permute-start(bf16[768,1024]{1,0:T(8,128)(2,1)} %bitcast.41), channel_id=1, source_target_pairs={{0,1},{1,0},{2,3},{3,2},{4,5},{5,4},{6,7},{7,6},{8,9},{9,8},{10,11... | collective-permute-start | bytes 4718600 | tf_op jit(solution)/shard_map/ppermute | solution.py:309
  35.7 2.2 %collective-permute-start.1 = (bf16[768,1024]{1,0:T(8,128)(2,1)}, bf16[768,1024]{1,0:T(8,128)(2,1)}, u32[]{:S(2)}, u32[]{:S(2)}) collective-permute-start(bf16[768,1024]{1,0:T(8,128)(2,1)} %bitcast.40), channel_id=1, source_target_pairs={{0,1},{1,0},{2,3},{3,2},{4,5},{5,4},{6,7},{7,6},{8,9},{9,8},{10,11... | collective-permute-start | bytes 4718600 | tf_op jit(solution)/shard_map/ppermute | solution.py:310
  38.0 1.0 fusion.6
  39.1 2.4 %collective-permute-done.1.second_hbm = bf16[768,1024]{1,0:T(8,128)(2,1)} collective-permute-done((bf16[768,1024]{1,0:T(8,128)(2,1)}, bf16[768,1024]{1,0:T(8,128)(2,1)}, u32[]{:S(2)}, u32[]{:S(2)}) %collective-permute-start.1) | collective-permute-done | bytes 1572896 | tf_op jit(solution)/shard_map/ppermute | solution.py:310
  41.5 10.1 %all-to-all-done = bf16[24,8,1536]{2,1,0:T(8,128)(2,1)S(1)} async-done(((bf16[24,8,1536]{2,1,0:T(8,128)(2,1)}), bf16[24,8,1536]{2,1,0:T(8,128)(2,1)S(1)}, u32[]{:S(2)}, u32[]{:S(2)}) %all-to-all-start) | async-done | bytes 589856 | tf_op jit(solution)/shard_map/all_to_all | solution.py:272
  51.6 1.3 fusion
  52.9 29.3 %all_to_all.20 = bf16[32,8,1536]{2,1,0:T(8,128)(2,1)S(1)} all-to-all(bf16[32,8,1536]{2,1,0:T(8,128)(2,1)S(1)} %fusion), channel_id=1, replica_groups=mesh['ep'=32,'grp'=24] {'ep'}, dimensions={0} | all-to-all | bytes 1572864 | tf_op jit(solution)/shard_map/all_to_all | solution.py:315
  82.4 6.5 %collective-permute-start.2 = (bf16[256,1536]{1,0:T(8,128)(2,1)S(1)}, bf16[256,1536]{1,0:T(8,128)(2,1)S(1)}, u32[]{:S(2)}, u32[]{:S(2)}) collective-permute-start(bf16[256,1536]{1,0:T(8,128)(2,1)S(1)} %bitcast_select_fusion.rows_hbm), channel_id=1, source_target_pairs={{0,1},{1,0},{2,3},{3,2},{4,5},{5,4},{6,7},{7,6},{8,9},{9,8},{10,11... | collective-permute-start | bytes 2359304 | tf_op jit(solution)/shard_map/ppermute | solution.py:320
  88.9 1.6 multiply_convert_fusion
  90.5 0.3 collective-permute-done.2.other_rows_hbm
  90.8 1.7 fusion.1.slope_hbm
  92.5 6.0 %grad.1 = bf16[12,2,4,32,1024]{4,3,2,1,0:T(8,128)(2,1)} custom-call(s32[1,24]{1,0:T(1,128)} %experts_ref.1, bf16[256,1536]{1,0:T(8,128)(2,1)} %copy-done, bf16[256,1024]{1,0:T(8,128)(2,1)} %fusion.1.slope_hbm, bf16[256,1024]{1,0:T(8,128)(2,1)} %get-tuple-element.28.act_hbm, bf16[256,1536]{1,0:T(8,128)(2,1)} %copy-done.2, ...), custom_call_target="tpu_custom_call", output_to_operand_aliasing={{}: (7, {})} | custom-call | tf_op jit(solution)/shard_map/grad/pallas_call | solution.py:326
  98.6 1.0 copy-done.3
  99.6 0.5 copy-done.6
  100.1 0.6 fusion.2
  100.8 18.3 %all_to_all.21 = bf16[32,8,768]{2,1,0:T(8,128)(2,1)} all-to-all(bf16[32,8,768]{2,1,0:T(8,128)(2,1)S(1)} %fusion.2), channel_id=1, replica_groups=mesh['ep'=32,'grp'=24] {'ep'}, dimensions={0} | all-to-all | bytes 786432 | tf_op jit(solution)/shard_map/all_to_all | solution.py:366
  119.1 2.0 %back_mid.1 = bf16[192,768]{1,0:T(8,128)(2,1)} custom-call(bf16[256,192]{1,0:T(8,128)(2,1)} %get-tuple-element.16.pick_ref, bf16[256,768]{1,0:T(8,128)(2,1)} %bitcast.35), custom_call_target="tpu_custom_call" | custom-call | tf_op jit(solution)/shard_map/back_mid/pallas_call | solution.py:369
  121.1 27.2 %all_to_all.22 = bf16[24,8,768]{2,1,0:T(8,128)(2,1)} all-to-all(bf16[24,8,768]{2,1,0:T(8,128)(2,1)} %bitcast.36), channel_id=1, replica_groups=mesh['ep'=32,'grp'=24] {'grp'}, dimensions={0} | all-to-all | bytes 589824 | tf_op jit(solution)/shard_map/all_to_all | solution.py:376
  148.3 1.9 back_own.1
  150.2 34.0 %reduce-scatter.2.cloned.1.call-done = bf16[256,1024]{1,0:T(8,128)(2,1)} async-done(((bf16[3072,1024]{1,0:T(8,128)(2,1)}), bf16[256,1024]{1,0:T(8,128)(2,1)}) %reduce-scatter.2.cloned.1.call-update) | async-done | bytes 524304 | tf_op jit(solution)/shard_map/reduce_scatter | solution.py:358
  (16 shorter events, 0.4 us)
Async XLA Ops:
  10.1 41.5 %all-to-all-start = ((bf16[24,8,1536]{2,1,0:T(8,128)(2,1)}), bf16[24,8,1536]{2,1,0:T(8,128)(2,1)S(1)}, u32[]{:S(2)}, u32[]{:S(2)}) async-start(bf16[24,8,1536]{2,1,0:T(8,128)(2,1)} %bitcast.38), calls=%async_computation | async-start | bytes 1179648 | tf_op jit(solution)/shard_map/all_to_all | solution.py:272
  26.8 157.4 %reduce-scatter.2.cloned.1.call-start = ((), (), s32[]{:S(2)}) async-start(), calls=%async_computation.5 | async-start | bytes 6815744 | tf_op jit(solution)/shard_map/reduce_scatter | solution.py:358
  33.6 5.5 %collective-permute-start = (bf16[768,1024]{1,0:T(8,128)(2,1)}, bf16[768,1024]{1,0:T(8,128)(2,1)S(1)}, u32[]{:S(2)}, u32[]{:S(2)}) collective-permute-start(bf16[768,1024]{1,0:T(8,128)(2,1)} %bitcast.41), channel_id=1, source_target_pairs={{0,1},{1,0},{2,3},{3,2},{4,5},{5,4},{6,7},{7,6},{8,9},{9,8},{10,11... | collective-permute-start | bytes 4718600 | tf_op jit(solution)/shard_map/ppermute | solution.py:309
  35.7 5.8 %collective-permute-start.1 = (bf16[768,1024]{1,0:T(8,128)(2,1)}, bf16[768,1024]{1,0:T(8,128)(2,1)}, u32[]{:S(2)}, u32[]{:S(2)}) collective-permute-start(bf16[768,1024]{1,0:T(8,128)(2,1)} %bitcast.40), channel_id=1, source_target_pairs={{0,1},{1,0},{2,3},{3,2},{4,5},{5,4},{6,7},{7,6},{8,9},{9,8},{10,11... | collective-permute-start | bytes 4718600 | tf_op jit(solution)/shard_map/ppermute | solution.py:310
  39.1 43.2 %copy-start.1 = (bf16[768,1024]{1,0:T(8,128)(2,1)}, bf16[768,1024]{1,0:T(8,128)(2,1)S(1)}, u32[]{:S(2)}) copy-start(bf16[768,1024]{1,0:T(8,128)(2,1)S(1)} %collective-permute-done.first_hbm) | copy-start | bytes 4718596
  52.9 36.0 %copy-start.5 = (bf16[1,1,768,1024]{3,2,1,0:T(8,128)(2,1)S(1)}, bf16[1,1,768,1024]{3,2,1,0:T(8,128)(2,1)}, u32[]{:S(2)}) copy-start(bf16[1,1,768,1024]{3,2,1,0:T(8,128)(2,1)} %param.14) | copy-start | bytes 4718596
  82.4 8.4 %copy-start = (bf16[256,1536]{1,0:T(8,128)(2,1)}, bf16[256,1536]{1,0:T(8,128)(2,1)S(1)}, u32[]{:S(2)}) copy-start(bf16[256,1536]{1,0:T(8,128)(2,1)S(1)} %bitcast_select_fusion.rows_hbm) | copy-start | bytes 2359300
  82.4 8.4 %copy-start.4 = (bf16[1,1,768,1024]{3,2,1,0:T(8,128)(2,1)S(1)}, bf16[1,1,768,1024]{3,2,1,0:T(8,128)(2,1)}, u32[]{:S(2)}) copy-start(bf16[1,1,768,1024]{3,2,1,0:T(8,128)(2,1)} %param.15) | copy-start | bytes 4718596
  82.4 8.4 %collective-permute-start.2 = (bf16[256,1536]{1,0:T(8,128)(2,1)S(1)}, bf16[256,1536]{1,0:T(8,128)(2,1)S(1)}, u32[]{:S(2)}, u32[]{:S(2)}) collective-permute-start(bf16[256,1536]{1,0:T(8,128)(2,1)S(1)} %bitcast_select_fusion.rows_hbm), channel_id=1, source_target_pairs={{0,1},{1,0},{2,3},{3,2},{4,5},{5,4},{6,7},{7,6},{8,9},{9,8},{10,11... | collective-permute-start | bytes 2359304 | tf_op jit(solution)/shard_map/ppermute | solution.py:320
  90.8 1.7 copy-start.2
  98.6 1.0 copy-start.3
  98.6 1.6 copy-start.6
Sparse Core Ops, SparseCore 0:
  98.7 85.4 reduce-scatter.1
